TPU v7x, 32 devices: a whole 2x2x4 slice. The times are simulated.
32 devices in a mesh: groups: 2 (over x), cache: 8 (over z, y), mp: 2 (over core).
Axes of the slice: x: 2, y: 2, z: 4, core: 2. Of those that a mesh axis runs over, the one named last changes fastest.
Arguments:
- acceptance_signal: bfloat16 [512, 2048], P(('groups', 'cache'), 'mp'), parts along dimension 0, may hold values from -6 to 6
- address_vectors: bfloat16 [512, 2048], P(('groups', 'cache'), 'mp'), parts along dimension 0, may hold values from -0.75 to 0.75
- payload_vectors: bfloat16 [512, 2048], P(('groups', 'cache'), 'mp'), parts along dimension 0, may hold values from -6 to 6
- logarithmic_fading: bfloat16 [512, 2048], P(('groups', 'cache'), 'mp'), parts along dimension 0, may hold values from -10 to 0
- presigmoid_switch: bfloat16 [512, 2048], P(('groups', 'cache'), 'mp'), parts along dimension 0, may hold values from -6 to 6
- diagonal_reward_coefficients: float32 [2048], P('mp'), may hold values from -4 to 4
- layernorm_scaling: float32 [2048], P('mp'), may hold values from 0.5 to 1.5
- layernorm_shift: float32 [2048], P('mp'), may hold values from -1.5 to 1.5
- stored_memory_matrices: float32 [80, 32, 4096], P(('groups', 'cache'), 'mp'), parts along dimension 0, may hold values from -3 to 3
- holder_location: int32 [80], P('groups'), parts along dimension 0, may hold values from 0 to 39, as said below
- conversation_label: int32 [64], P(('groups', 'cache')), parts along dimension 0, may hold values from 0 to 39, as said below
- fresh_entry_amounts: int32 [64], P(('groups', 'cache')), parts along dimension 0, may hold values from 1 to 8, as said below
Outputs:
- time_mixed: bfloat16 [512, 2048], P(('groups', 'cache'), 'mp'), parts along dimension 0
- updated_store: float32 [80, 32, 4096], P(('groups', 'cache'), 'mp'), parts along dimension 0
There are 2 independent parts, one for each index of `groups`. A program takes and returns all parts, laid end to end along the dimension named above; an argument that names none is the same for every part. Nothing has to cross between parts.
Inputs may be any that keep to these rules, and one draw needn't show every extreme that they name: A permutation: session s's state is row holder_location[s] of stored_memory_matrices, held by the owner holder_location[s] // 5. `conversation_label`: distinct sessions; the 4 sessions of one device lie with 4 distinct owners; one owner holds up to 5 served sessions, and in every draw some owner holds exactly 5. `fresh_entry_amounts`: in every draw some device's sessions all have 8 tokens.
All inputs are finite; a program needn't handle non-finite values.
Results may differ from a plain program's by a relative error of at most 0.001.
Values may be sent and summed in bfloat16 or wider, within the bound.
No kernel may reach another device: no remote copies, remote signals or barrier semaphores. Data moves between devices by JAX's collectives and lax.ppermute only.
A program may use at most 128 MiB of HBM per device.

v0:
```python
import jax
import jax.numpy as jnp
from jax import lax
from jax.sharding import PartitionSpec as P

GROUP_WIDTH = 64


EPS = 0.00064


def time_mix(
    recv_in,
    key_in,
    value_in,
    decay_in,
    gate_in,
    start_state,
    counts,
    diagonal_reward_coefficients,
    layernorm_scaling,
    layernorm_shift,
):
    sessions, length, channels = recv_in.shape
    group_ordinal = channels // GROUP_WIDTH

    def split_heads(tensor):
        return tensor.astype(jnp.float32).reshape(sessions, length, group_ordinal, GROUP_WIDTH)

    acceptance_vectors = split_heads(recv_in)
    address_by_group = split_heads(key_in)
    value_heads = split_heads(value_in)
    log_decay = -jnp.exp(split_heads(decay_in))
    cumulative = jnp.cumsum(log_decay, axis=1)
    exclusive = cumulative - log_decay
    positions = jnp.arange(length, dtype=jnp.int32)
    valid_rows = positions[None, :] < counts[:, None]
    r_decayed = acceptance_vectors * jnp.exp(exclusive)
    k_decayed = address_by_group * jnp.exp(-cumulative)
    scores = jnp.einsum("qthd,qshd->qhts", r_decayed, k_decayed, precision=lax.Precision.HIGHEST)
    strictly_below = positions[:, None] > positions[None, :]
    scores = jnp.where(strictly_below[None, None], scores, 0.0)
    diagonal_reward_array = diagonal_reward_coefficients.reshape(group_ordinal, GROUP_WIDTH)
    diagonal_contribution = jnp.sum(
        acceptance_vectors * diagonal_reward_array * address_by_group, axis=3
    )
    wkv = jnp.einsum("qhts,qshd->qthd", scores, value_heads, precision=lax.Precision.HIGHEST)
    wkv = wkv + diagonal_contribution[..., None] * value_heads
    wkv = wkv + jnp.einsum(
        "qthi,qhij->qthj", r_decayed, start_state, precision=lax.Precision.HIGHEST
    )
    last_row = (positions[None, :] == counts[:, None] - 1).astype(jnp.float32)
    last_cum = jnp.einsum("ql,qlhd->qhd", last_row, cumulative, precision=lax.Precision.HIGHEST)
    carry_gap = jnp.minimum(last_cum[:, None] - cumulative, 0.0)
    k_carried = (
        address_by_group * jnp.exp(carry_gap) * valid_rows[:, :, None, None].astype(jnp.float32)
    )
    final_state = jnp.exp(last_cum)[..., None] * start_state
    final_state = final_state + jnp.einsum(
        "qshi,qshj->qhij", k_carried, value_heads, precision=lax.Precision.HIGHEST
    )
    centred = wkv - jnp.mean(wkv, axis=3, keepdims=True)
    variance = jnp.mean(centred * centred, axis=3, keepdims=True)
    normed = centred * lax.rsqrt(variance + EPS) * layernorm_scaling.reshape(
        group_ordinal, GROUP_WIDTH
    ) + layernorm_shift.reshape(group_ordinal, GROUP_WIDTH)
    gated_rows = normed.reshape(sessions, length, channels) * jax.nn.silu(
        gate_in.astype(jnp.float32)
    )
    mixed_rows = jnp.where(valid_rows[:, :, None], gated_rows, 0.0).astype(jnp.bfloat16)
    return (mixed_rows, final_state.reshape(sessions, group_ordinal, GROUP_WIDTH * GROUP_WIDTH))


def shards(
    acceptance_signal,
    address_vectors,
    payload_vectors,
    logarithmic_fading,
    presigmoid_switch,
    diagonal_reward_coefficients,
    layernorm_scaling,
    layernorm_shift,
    stored_memory_matrices,
    holder_location,
    conversation_label,
    fresh_entry_amounts,
):
    devices = lax.axis_size("cache")
    myself = lax.axis_index("cache")
    sess_here = conversation_label.shape[0]
    store_rows = stored_memory_matrices.shape[0]
    heads_here = stored_memory_matrices.shape[1]
    length = acceptance_signal.shape[0] // sess_here
    channels = acceptance_signal.shape[1]
    every_id, every_count = (
        lax.all_gather(conversation_label, "cache", axis=0, tiled=True),
        lax.all_gather(fresh_entry_amounts, "cache", axis=0, tiled=True),
    )
    every_slot = holder_location[every_id].reshape(devices, sess_here)
    mine_mask = every_slot // store_rows == myself
    wanted = jnp.any(mine_mask, axis=1)
    wanted_row = jnp.sum(jnp.where(mine_mask, every_slot % store_rows, 0), axis=1)
    my_owner = holder_location[conversation_label] // store_rows
    owner_index = jnp.arange(devices, dtype=jnp.int32)
    recv_rows = acceptance_signal.reshape(sess_here, length, channels)
    key_rows = address_vectors.reshape(sess_here, length, channels)
    value_rows = payload_vectors.reshape(sess_here, length, channels)
    decay_rows = logarithmic_fading.reshape(sess_here, length, channels)
    gate_rows = presigmoid_switch.reshape(sess_here, length, channels)
    has_session = owner_index[:, None] == my_owner[None, :]
    source_row = jnp.sum(
        jnp.where(has_session, jnp.arange(sess_here, dtype=jnp.int32)[None, :], 0), axis=1
    )
    filled = jnp.any(has_session, axis=1)[:, None, None]
    zero_value = jnp.zeros((), jnp.bfloat16)
    out_recv = jnp.where(filled, recv_rows[source_row], zero_value)
    out_key = jnp.where(filled, key_rows[source_row], zero_value)
    out_value = jnp.where(filled, value_rows[source_row], zero_value)
    out_decay = jnp.where(filled, decay_rows[source_row], zero_value)
    out_gate = jnp.where(filled, gate_rows[source_row], zero_value)
    shipped = (
        lax.all_to_all(out_recv, "cache", split_axis=0, concat_axis=0, tiled=True),
        lax.all_to_all(out_key, "cache", split_axis=0, concat_axis=0, tiled=True),
        lax.all_to_all(out_value, "cache", split_axis=0, concat_axis=0, tiled=True),
        lax.all_to_all(out_decay, "cache", split_axis=0, concat_axis=0, tiled=True),
        lax.all_to_all(out_gate, "cache", split_axis=0, concat_axis=0, tiled=True),
    )
    capacity = min(devices, store_rows)
    serve_order = jnp.argsort(jnp.where(wanted, owner_index, devices + owner_index))[:capacity]
    counts_here = jnp.sum(jnp.where(mine_mask, every_count.reshape(devices, sess_here), 0), axis=1)
    counts_here = jnp.where(wanted, counts_here, 0)
    start_state = stored_memory_matrices[wanted_row[serve_order]].reshape(
        capacity, heads_here, GROUP_WIDTH, GROUP_WIDTH
    )
    mixed_rows, final_state = time_mix(
        shipped[0][serve_order],
        shipped[1][serve_order],
        shipped[2][serve_order],
        shipped[3][serve_order],
        shipped[4][serve_order],
        start_state,
        counts_here[serve_order],
        diagonal_reward_coefficients,
        layernorm_scaling,
        layernorm_shift,
    )
    back_rows = jnp.zeros((devices, length, channels), jnp.bfloat16).at[serve_order].set(mixed_rows)
    returned = lax.all_to_all(back_rows, "cache", split_axis=0, concat_axis=0, tiled=True)
    result = returned[my_owner]
    target = jnp.where(wanted[serve_order], wanted_row[serve_order], store_rows)
    updated_store = stored_memory_matrices.at[target].set(final_state, mode="drop")
    return (result.reshape(sess_here * length, channels), updated_store)


def solution(mesh):
    in_specs = (
        P(("groups", "cache"), "mp"),
        P(("groups", "cache"), "mp"),
        P(("groups", "cache"), "mp"),
        P(("groups", "cache"), "mp"),
        P(("groups", "cache"), "mp"),
        P("mp"),
        P("mp"),
        P("mp"),
        P(("groups", "cache"), "mp", None),
        P("groups"),
        P(("groups", "cache")),
        P(("groups", "cache")),
    )
    out_specs = (P(("groups", "cache"), "mp"), P(("groups", "cache"), "mp", None))
    return jax.shard_map(shards, mesh=mesh, in_specs=in_specs, out_specs=out_specs, check_vma=False)
```

profile of v0, /device:TPU:0, one launch (start us, length us, event | category | flops | bytes accessed | tf_op | source)
XLA Modules:
  0.0 104.8 jit_solution(4082770132147598320)
XLA Ops:
  0.7 1.4 %copy.55 = f32[5,16,4096]{2,1,0:T(8,128)S(1)} copy(f32[5,16,4096]{2,1,0:T(8,128)} %param.20) | data formatting | bytes 2621440
  6.9 7.3 %all-to-all-start.3 = ((bf16[8,8,1024]{2,1,0:T(8,128)(2,1)}), bf16[8,8,1024]{2,1,0:T(8,128)(2,1)S(1)}, u32[]{:S(2)}, u32[]{:S(2)}) async-start(bf16[8,8,1024]{2,1,0:T(8,128)(2,1)} %get-tuple-element.24), calls=%async_computation.3 | async-start | bytes 262144 | tf_op jit(solution)/shard_map/all_to_all | solution.py:123
  15.9 11.9 %all-reduce.2 = (s32[32]{0:T(128)S(1)}, s32[32]{0:T(128)S(1)}) all-reduce(s32[32]{0:T(128)S(1)} %dynamic-update-slice, s32[32]{0:T(128)S(1)} %dynamic-update-slice.1), channel_id=1, replica_groups=mesh['groups'=2,'cache'=8,'mp'=2] {'cache'}, use_global_device_ids=true, to_apply=%add | all-reduce | flops 64 | bytes 512
  33.3 3.4 %all-to-all-start.2 = ((bf16[8,8,1024]{2,1,0:T(8,128)(2,1)}), bf16[8,8,1024]{2,1,0:T(8,128)(2,1)S(1)}, u32[]{:S(2)}, u32[]{:S(2)}) async-start(bf16[8,8,1024]{2,1,0:T(8,128)(2,1)} %get-tuple-element.23), calls=%async_computation.2 | async-start | bytes 262144 | tf_op jit(solution)/shard_map/all_to_all | solution.py:125
  37.3 1.7 %gather_fusion.12 = f32[5,16,4096]{2,1,0:T(8,128)} fusion(f32[5,16,4096]{2,1,0:T(8,128)S(1)} %copy.55, s32[1024]{0:T(1024)S(1)} %pad_clamp_fusion.1), kind=kCustom, calls=%fused_computation.12 | custom fusion | bytes 2621460 | tf_op jit(solution)/shard_map/gather | solution.py:132
  39.0 2.3 %reshape.245 = f32[5,16,64,64]{3,2,1,0:T(8,128)S(1)} reshape(f32[5,16,4096]{2,1,0:T(8,128)} %gather_fusion.12) | data formatting | bytes 2621440 | tf_op jit(solution)/shard_map/reshape | solution.py:132
  44.7 5.9 %all-to-all-start.1 = ((bf16[8,8,1024]{2,1,0:T(8,128)(2,1)}), bf16[8,8,1024]{2,1,0:T(8,128)(2,1)S(1)}, u32[]{:S(2)}, u32[]{:S(2)}) async-start(bf16[8,8,1024]{2,1,0:T(8,128)(2,1)} %get-tuple-element.22), calls=%async_computation.1 | async-start | bytes 262144 | tf_op jit(solution)/shard_map/all_to_all | solution.py:122
  51.4 6.6 %all-to-all-done.1 = bf16[8,8,1024]{2,1,0:T(8,128)(2,1)S(1)} async-done(((bf16[8,8,1024]{2,1,0:T(8,128)(2,1)}), bf16[8,8,1024]{2,1,0:T(8,128)(2,1)S(1)}, u32[]{:S(2)}, u32[]{:S(2)}) %all-to-all-start.1) | async-done | bytes 131104 | tf_op jit(solution)/shard_map/all_to_all | solution.py:122
  58.0 3.4 %all-to-all-start = ((bf16[8,8,1024]{2,1,0:T(8,128)(2,1)}), bf16[8,8,1024]{2,1,0:T(8,128)(2,1)S(1)}, u32[]{:S(2)}, u32[]{:S(2)}) async-start(bf16[8,8,1024]{2,1,0:T(8,128)(2,1)} %get-tuple-element.25), calls=%async_computation | async-start | bytes 262144 | tf_op jit(solution)/shard_map/all_to_all | solution.py:124
  62.8 1.2 %fusion.29 = f32[5,8,16,64]{3,2,1,0:T(8,128)S(1)} fusion(f32[5,8,16,64]{3,2,1,0:T(8,128)S(1)} %neg.14), kind=kOutput, calls=%fused_computation.100 | output fusion | flops 286720 | bytes 327680 | tf_op jit(solution)/shard_map/jit(cumsum)/reduce_window_sum | solution.py:34
  64.1 4.6 %all-to-all-done = bf16[8,8,1024]{2,1,0:T(8,128)(2,1)S(1)} async-done(((bf16[8,8,1024]{2,1,0:T(8,128)(2,1)}), bf16[8,8,1024]{2,1,0:T(8,128)(2,1)S(1)}, u32[]{:S(2)}, u32[]{:S(2)}) %all-to-all-start) | async-done | bytes 131104 | tf_op jit(solution)/shard_map/all_to_all | solution.py:124
  68.7 4.0 %all-to-all-start.4 = ((bf16[8,8,1024]{2,1,0:T(8,128)(2,1)}), bf16[8,8,1024]{2,1,0:T(8,128)(2,1)}, u32[]{:S(2)}, u32[]{:S(2)}) async-start(bf16[8,8,1024]{2,1,0:T(8,128)(2,1)} %get-tuple-element.21), calls=%async_computation.4 | async-start | bytes 262144 | tf_op jit(solution)/shard_map/all_to_all | solution.py:126
  72.7 1.2 %gather_fusion.4 = bf16[5,8,1024]{2,1,0:T(8,128)(2,1)} fusion(bf16[8,8,1024]{2,1,0:T(8,128)(2,1)S(1)} %all-to-all-done, s32[1024]{0:T(1024)S(1)} %pad_clamp_fusion.4), kind=kCustom, calls=%fused_computation.4 | custom fusion | bytes 163860 | tf_op jit(solution)/shard_map/gather | solution.py:138
  73.9 1.1 %reshape.241 = bf16[5,8,16,64]{3,2,1,0:T(8,128)(2,1)S(1)} reshape(bf16[5,8,1024]{2,1,0:T(8,128)(2,1)} %gather_fusion.4) | data formatting | bytes 163840 | tf_op jit(solution)/shard_map/reshape | solution.py:28
  75.3 2.8 %multiply_multiply_fusion = (f32[5,8,16,64]{3,2,1,0:T(8,128)}, f32[5,8,16,64]{3,2,1,0:T(8,128)}, f32[5,8,16,64]{3,2,1,0:T(8,128)S(1)}, f32[5,8,16]{2,1,0:T(8,128)}) fusion(f32[5,8,16,64]{3,2,1,0:T(8,128)} %reshape.251, f32[5,8,16,64]{3,2,1,0:T(8,128)} %copy-done.5, f32[5,8]{1,0:T(8,128)} %get-tuple-element.15, f32[5,16,64]{2,1,0:T(8,128)S(1)} %bitcast.59, ...), kind=kLoop, calls=%fused_computation.29 | loop fusion | flops 449920 | bytes 1174176 | tf_op jit(solution)/shard_map/mul | solution.py:56
  78.2 1.4 %copy.23 = f32[5,8,16]{1,2,0:T(8,128)} copy(f32[5,8,16]{2,1,0:T(8,128)} %get-tuple-element.14) | data formatting | bytes 5120 | tf_op jit(solution)/shard_map/reduce_sum | solution.py:44
  79.6 2.4 %convolution_bitcast_fusion = f32[5,8,16,64]{3,1,2,0:T(8,128)S(1)} fusion(f32[5,16,64,64]{3,2,1,0:T(8,128)S(1)} %reshape.245, f32[5,8,16,64]{3,2,1,0:T(8,128)S(1)} %get-tuple-element.13), kind=kOutput, calls=%fused_computation.20 | convolution fusion | flops 31457280 | bytes 1638400 | tf_op jit(solution)/shard_map/qthi,qhij->qthj/dot_general | solution.py:49
  84.8 1.6 %gather_fusion.14 = bf16[5,8,1024]{2,1,0:T(8,128)(2,1)S(1)} fusion(bf16[8,8,1024]{2,1,0:T(8,128)(2,1)} %all-to-all-done.4, s32[1024]{0:T(1024)} %copy-done.14), kind=kCustom, calls=%fused_computation.14 | custom fusion | bytes 163860 | tf_op jit(solution)/shard_map/gather | solution.py:140
  86.4 1.0 fusion.13
  88.1 2.1 %scatter_fusion = bf16[8,8,1024]{2,1,0:T(8,128)(2,1)} fusion(bf16[8,8,1024]{2,1,0:T(8,128)(2,1)} %broadcast_in_dim.118, s32[5]{0:T(128)} %copy-done.18, bf16[5,8,1024]{2,1,0:T(8,128)(2,1)S(1)} %fusion.13), kind=kCustom, calls=%fused_computation.17 | custom fusion | bytes 245780 | tf_op jit(solution)/shard_map/scatter | solution.py:147
  90.2 5.9 %all-to-all-start.5 = ((bf16[8,8,1024]{2,1,0:T(8,128)(2,1)}), bf16[8,8,1024]{2,1,0:T(8,128)(2,1)S(1)}, u32[]{:S(2)}, u32[]{:S(2)}) async-start(bf16[8,8,1024]{2,1,0:T(8,128)(2,1)} %scatter_fusion), calls=%async_computation.5 | async-start | bytes 262144 | tf_op jit(solution)/shard_map/all_to_all | solution.py:148
  96.1 4.0 %multiply_add_fusion = f32[5,16,64,64]{3,2,1,0:T(8,128)} fusion(f32[5,16,64,64]{3,2,1,0:T(8,128)S(1)} %reshape.245, f32[5,16,64]{2,1,0:T(8,128)S(1)} %exp.24, f32[5,8,16,64]{3,2,1,0:T(8,128)S(1)} %copy-done.6, bf16[5,8,16,64]{3,2,1,0:T(8,128)(2,1)S(1)} %reshape.241), kind=kOutput, calls=%fused_computation.19 | convolution fusion | flops 32112640 | bytes 2887680 | tf_op jit(solution)/shard_map/qshi,qshj->qhij/dot_general | solution.py:59
  100.2 2.4 %reshape.400 = f32[5,16,4096]{2,1,0:T(8,128)S(1)} reshape(f32[5,16,64,64]{3,2,1,0:T(8,128)} %multiply_add_fusion) | data formatting | bytes 2621440 | tf_op jit(solution)/shard_map/reshape | solution.py:71
  103.5 1.3 %gather_fusion.15 = bf16[4,8,1024]{2,1,0:T(8,128)(2,1)} fusion(bf16[8,8,1024]{2,1,0:T(8,128)(2,1)S(1)} %all-to-all-done.5, s32[1024]{0:T(1024)} %pad_clamp_fusion), kind=kCustom, calls=%fused_computation.15 | custom fusion | bytes 131088 | tf_op jit(solution)/shard_map/gather | solution.py:149
  (120 shorter events, 22.2 us)
Async XLA Ops:
  0.6 2.4 %copy-start = (bf16[32,1024]{1,0:T(8,128)(2,1)S(1)}, bf16[32,1024]{1,0:T(8,128)(2,1)}, u32[]{:S(2)}) copy-start(bf16[32,1024]{1,0:T(8,128)(2,1)} %param.16) | copy-start | bytes 196612
  0.6 3.0 %copy-start.8 = (bf16[32,1024]{1,0:T(8,128)(2,1)S(1)}, bf16[32,1024]{1,0:T(8,128)(2,1)}, u32[]{:S(2)}) copy-start(bf16[32,1024]{1,0:T(8,128)(2,1)} %param.12) | copy-start | bytes 196612
  0.7 3.6 %copy-start.9 = (bf16[32,1024]{1,0:T(8,128)(2,1)S(1)}, bf16[32,1024]{1,0:T(8,128)(2,1)}, u32[]{:S(2)}) copy-start(bf16[32,1024]{1,0:T(8,128)(2,1)} %param.15) | copy-start | bytes 196612
  2.1 35.2 %copy-start.2 = (f32[5,16,4096]{2,1,0:T(8,128)}, f32[5,16,4096]{2,1,0:T(8,128)S(1)}, u32[]{:S(2)}) copy-start(f32[5,16,4096]{2,1,0:T(8,128)S(1)} %copy.55) | copy-start | bytes 3932164
  2.1 2.7 %copy-start.10 = (bf16[32,1024]{1,0:T(8,128)(2,1)S(1)}, bf16[32,1024]{1,0:T(8,128)(2,1)}, u32[]{:S(2)}) copy-start(bf16[32,1024]{1,0:T(8,128)(2,1)} %param.13) | copy-start | bytes 196612
  2.1 3.3 %copy-start.11 = (bf16[32,1024]{1,0:T(8,128)(2,1)S(1)}, bf16[32,1024]{1,0:T(8,128)(2,1)}, u32[]{:S(2)}) copy-start(bf16[32,1024]{1,0:T(8,128)(2,1)} %param.14) | copy-start | bytes 196612
  3.6 10.6 %copy-start.23 = (u32[32]{0:T(128)S(1)}, u32[32]{0:T(128)}, u32[]{:S(2)}) copy-start(u32[32]{0:T(128)} %constant.73) | copy-start | bytes 388
  3.6 12.0 %copy-start.22 = (s32[4]{0:T(128)S(1)}, s32[4]{0:T(128)}, u32[]{:S(2)}) copy-start(s32[4]{0:T(128)} %param.23) | copy-start | bytes 52
  6.9 26.4 %all-to-all-start.3 = ((bf16[8,8,1024]{2,1,0:T(8,128)(2,1)}), bf16[8,8,1024]{2,1,0:T(8,128)(2,1)S(1)}, u32[]{:S(2)}, u32[]{:S(2)}) async-start(bf16[8,8,1024]{2,1,0:T(8,128)(2,1)} %get-tuple-element.24), calls=%async_computation.3 | async-start | bytes 262144 | tf_op jit(solution)/shard_map/all_to_all | solution.py:123
  30.1 3.2 %copy-start.18 = (s32[5]{0:T(128)}, s32[5]{0:T(128)S(1)}, u32[]{:S(2)}) copy-start(s32[5]{0:T(128)S(1)} %compare_select_fusion.5) | copy-start | bytes 64
  30.1 42.6 %copy-start.14 = (s32[1024]{0:T(1024)}, s32[1024]{0:T(1024)S(1)}, u32[]{:S(2)}) copy-start(s32[1024]{0:T(1024)S(1)} %pad_clamp_fusion.4) | copy-start | bytes 12292
  33.3 11.4 %all-to-all-start.2 = ((bf16[8,8,1024]{2,1,0:T(8,128)(2,1)}), bf16[8,8,1024]{2,1,0:T(8,128)(2,1)S(1)}, u32[]{:S(2)}, u32[]{:S(2)}) async-start(bf16[8,8,1024]{2,1,0:T(8,128)(2,1)} %get-tuple-element.23), calls=%async_computation.2 | async-start | bytes 262144 | tf_op jit(solution)/shard_map/all_to_all | solution.py:125
  39.0 2.9 %copy-start.16 = (f32[1024]{0:T(1024)S(1)}, f32[1024]{0:T(1024)}, u32[]{:S(2)}) copy-start(f32[1024]{0:T(1024)} %param.19) | copy-start | bytes 12292
  39.0 3.0 %copy-start.17 = (f32[1024]{0:T(1024)S(1)}, f32[1024]{0:T(1024)}, u32[]{:S(2)}) copy-start(f32[1024]{0:T(1024)} %param.18) | copy-start | bytes 12292
  44.7 13.3 %all-to-all-start.1 = ((bf16[8,8,1024]{2,1,0:T(8,128)(2,1)}), bf16[8,8,1024]{2,1,0:T(8,128)(2,1)S(1)}, u32[]{:S(2)}, u32[]{:S(2)}) async-start(bf16[8,8,1024]{2,1,0:T(8,128)(2,1)} %get-tuple-element.22), calls=%async_computation.1 | async-start | bytes 262144 | tf_op jit(solution)/shard_map/all_to_all | solution.py:122
  58.0 10.7 %all-to-all-start = ((bf16[8,8,1024]{2,1,0:T(8,128)(2,1)}), bf16[8,8,1024]{2,1,0:T(8,128)(2,1)S(1)}, u32[]{:S(2)}, u32[]{:S(2)}) async-start(bf16[8,8,1024]{2,1,0:T(8,128)(2,1)} %get-tuple-element.25), calls=%async_computation | async-start | bytes 262144 | tf_op jit(solution)/shard_map/all_to_all | solution.py:124
  64.1 11.3 %copy-start.5 = (f32[5,8,16,64]{3,2,1,0:T(8,128)}, f32[5,8,16,64]{3,2,1,0:T(8,128)S(1)}, u32[]{:S(2)}) copy-start(f32[5,8,16,64]{3,2,1,0:T(8,128)S(1)} %fusion.29) | copy-start | bytes 491524
  68.7 16.1 %all-to-all-start.4 = ((bf16[8,8,1024]{2,1,0:T(8,128)(2,1)}), bf16[8,8,1024]{2,1,0:T(8,128)(2,1)}, u32[]{:S(2)}, u32[]{:S(2)}) async-start(bf16[8,8,1024]{2,1,0:T(8,128)(2,1)} %get-tuple-element.21), calls=%async_computation.4 | async-start | bytes 262144 | tf_op jit(solution)/shard_map/all_to_all | solution.py:126
  79.6 2.4 %copy-start.20 = (pred[8,8]{1,0:T(8,128)(4,1)S(1)}, pred[8,8]{1,0:T(8,128)(4,1)}, u32[]{:S(2)}) copy-start(pred[8,8]{1,0:T(8,128)(4,1)} %iota_compare_fusion.1) | copy-start | bytes 196
  79.6 3.3 %copy-start.12 = (f32[5,8,16]{1,2,0:T(8,128)S(1)}, f32[5,8,16]{1,2,0:T(8,128)}, u32[]{:S(2)}) copy-start(f32[5,8,16]{1,2,0:T(8,128)} %copy.23) | copy-start | bytes 7684
  83.9 12.2 %copy-start.6 = (f32[5,8,16,64]{3,2,1,0:T(8,128)S(1)}, f32[5,8,16,64]{3,2,1,0:T(8,128)}, u32[]{:S(2)}) copy-start(f32[5,8,16,64]{3,2,1,0:T(8,128)} %get-tuple-element.11) | copy-start | bytes 491524
  90.2 13.3 %all-to-all-start.5 = ((bf16[8,8,1024]{2,1,0:T(8,128)(2,1)}), bf16[8,8,1024]{2,1,0:T(8,128)(2,1)S(1)}, u32[]{:S(2)}, u32[]{:S(2)}) async-start(bf16[8,8,1024]{2,1,0:T(8,128)(2,1)} %scatter_fusion), calls=%async_computation.5 | async-start | bytes 262144 | tf_op jit(solution)/shard_map/all_to_all | solution.py:148
  100.2 2.4 %copy-start.3 = (f32[5,16,4096]{2,1,0:T(8,128)S(1)}, f32[5,16,4096]{2,1,0:T(8,128)}, u32[]{:S(2)}) copy-start(f32[5,16,4096]{2,1,0:T(8,128)} %copy-done.2) | copy-start | bytes 3932164
  100.2 2.4 %copy-start.19 = (s32[5]{0:T(128)S(1)}, s32[5]{0:T(128)}, u32[]{:S(2)}) copy-start(s32[5]{0:T(128)} %get-tuple-element.17) | copy-start | bytes 64
  (6 other events, 10.6 us)
where the time goes:
time: 106 us; the launch traced here: 105 us
  local copies, waits for them, and re-layouts  31.3 us (30%)
  starting transfers between devices  29.9 us (28%)
  blocking collectives  11.9 us (11%)
  waiting for transfers between devices  11.3 us (11%)
  other arithmetic  10.6 us (10%)
  matrix products  8.09 us (8%)
  between operations  1.81 us (2%)
    unnamed x1, blocking collectives  11.9 us
    all_to_all x1, starting transfers between devices, shards(): lax.all_to_all(out_key, 'cache', split_axis=0, concat_axis=0, tiled=True)  7.31 us
    all_to_all x1, waiting for transfers between devices, shards(): lax.all_to_all(out_recv, 'cache', split_axis=0, concat_axis=0, tiled=True)  6.63 us
    all_to_all x1, starting transfers between devices, shards(): lax.all_to_all(out_recv, 'cache', split_axis=0, concat_axis=0, tiled=True)  5.93 us
    all_to_all x1, starting transfers between devices, shards(): lax.all_to_all(back_rows, 'cache', split_axis=0, concat_axis=0, tiled=True)  5.9 us
    all_to_all x1, waiting for transfers between devices, shards(): lax.all_to_all(out_value, 'cache', split_axis=0, concat_axis=0, tiled=True)  4.62 us
    dot_general x1, matrix products, time_mix(): jnp.einsum('qshi,qshj->qhij', k_carried, value_heads, precision=lax.Preci...  4.01 us
    all_to_all x1, starting transfers between devices, shards(): lax.all_to_all(out_gate, 'cache', split_axis=0, concat_axis=0, tiled=True)  3.99 us
  transfers between devices with their start and end apart: 6, of which 2 were waited for; matrix products, arithmetic and copies ran while one was open for 35% of the time, Pallas kernels for 0%

commit v1 on v0

v1 whole, which is shorter than its diff:
```python
import functools

import jax
import jax.numpy as jnp
from jax import lax
from jax.experimental import pallas as pl
from jax.experimental.pallas import tpu as pltpu
from jax.sharding import PartitionSpec as P

GROUP_WIDTH = 64
EPS = 0.00064
LANES = 128
META = 128
F32 = jnp.float32
BF16 = jnp.bfloat16

SMEM = functools.partial(pl.BlockSpec, memory_space=pltpu.SMEM)
VMEM = functools.partial(pl.BlockSpec, memory_space=pltpu.VMEM)


def lane_ids(rows):
    return lax.broadcasted_iota(jnp.int32, (rows, LANES), 1)


def row_ids(rows):
    return lax.broadcasted_iota(jnp.int32, (rows, LANES), 0)


def place_of(hold, label, j, store_rows):
    location = hold[label[j]]
    owner = lax.div(location, jnp.int32(store_rows))
    return owner, location - owner * store_rows


def running_decay(w_tile):
    step = -jnp.exp(w_tile.astype(F32))
    rows = row_ids(step.shape[0])
    total = step
    shift = 1
    while shift < step.shape[0]:
        total = total + jnp.where(rows >= shift, pltpu.roll(total, shift, 0), 0.0)
        shift *= 2
    return step, total


def half_sums(x, low):
    first = jnp.sum(jnp.where(low, x, 0.0), axis=1, keepdims=True)
    second = jnp.sum(jnp.where(low, 0.0, x), axis=1, keepdims=True)
    return jnp.where(low, first, second)


def pack_kernel(store_rows, hold, label, count, r, k, v, w, out):
    devices, length, _ = out.shape
    channels = r.shape[1]
    lanes = lane_ids(length)
    for d in range(devices):
        out[d, :, 4 * channels :] = jnp.zeros((length, META), BF16)
    for j in range(label.shape[0]):
        owner, local = place_of(hold, label, j, store_rows)
        rows = pl.ds(j * length, length)
        for index, ref in enumerate((r, k, v, w)):
            out[owner, :, index * channels : (index + 1) * channels] = ref[rows, :]
        meta = jnp.where(lanes == 0, local + 1, jnp.where(lanes == 1, count[j], 0))
        out[owner, :, 4 * channels :] = meta.astype(F32).astype(BF16)


def meta_of(recv, source, base):
    tile = recv[source, :, base:].astype(F32)
    lanes = lane_ids(tile.shape[0])
    row = jnp.max(jnp.where(lanes == 0, tile, 0.0)).astype(jnp.int32) - 1
    return row, jnp.max(jnp.where(lanes == 1, tile, 0.0)).astype(jnp.int32)


def spread(scratch, column, tile, low, both):
    length = tile.shape[0]
    turned = pltpu.roll(tile, GROUP_WIDTH, 1)
    even = jnp.where(low, tile, turned) if both else tile
    odd = jnp.where(low, turned, tile) if both else turned
    scratch[pl.ds(2 * column * length, length), :] = even
    scratch[pl.ds((2 * column + 1) * length, length), :] = odd


def token_rows(length, group, t):
    return pl.ds(group * 8 * length + t, 8, stride=length)


def take(x, index):
    return jnp.take_along_axis(x, index, axis=1, mode="promise_in_bounds")


def state_read_kernel(recv, store, out, scratch, result):
    devices, length, channels = out.shape
    columns = channels // LANES
    groups = store.shape[1] // 8
    tiles = store.shape[2] // LANES
    low = lane_ids(length) < GROUP_WIDTH
    low8 = lane_ids(8) < GROUP_WIDTH
    half = jnp.where(low8, 0, 1)

    @pl.loop(0, devices)
    def _(source):
        row, _ = meta_of(recv, source, 4 * channels)

        @pl.when(row >= 0)
        def _():
            for c in range(columns):
                at = c * LANES
                step, total = running_decay(recv[source, :, 3 * channels + at : 3 * channels + at + LANES])
                decayed = recv[source, :, at : at + LANES].astype(F32) * jnp.exp(total - step)
                spread(scratch, c, decayed, low, False)
            for g in range(groups):
                queries = [scratch[token_rows(length, g, t), :] for t in range(length)]
                sums = [jnp.zeros((8, LANES), F32) for _ in range(length)]
                for tile in range(tiles):
                    state = store[row, g * 8 : g * 8 + 8, tile * LANES : (tile + 1) * LANES]
                    index = half + 2 * tile
                    for t in range(length):
                        sums[t] = sums[t] + take(queries[t], index) * state
                for t in range(length):
                    result[token_rows(length, g, t), :] = sums[t] + pltpu.roll(sums[t], GROUP_WIDTH, 1)
            for c in range(columns):
                even = result[2 * c * length : (2 * c + 1) * length, :]
                odd = result[(2 * c + 1) * length : (2 * c + 2) * length, :]
                out[source, :, c * LANES : (c + 1) * LANES] = jnp.where(low, even, odd)


def state_write_kernel(recv, after, store, out, keys, values, decays):
    del after
    devices, length, width = recv.shape
    channels = (width - META) // 4
    columns = channels // LANES
    groups = store.shape[1] // 8
    tiles = store.shape[2] // LANES
    low = lane_ids(length) < GROUP_WIDTH
    rows = row_ids(length)
    half = jnp.where(lane_ids(8) < GROUP_WIDTH, 0, 1)
    out[...] = store[...]

    @pl.loop(0, devices)
    def _(source):
        row, count = meta_of(recv, source, 4 * channels)

        @pl.when(row >= 0)
        def _():
            for c in range(columns):
                at = c * LANES
                _, total = running_decay(recv[source, :, 3 * channels + at : 3 * channels + at + LANES])
                last = jnp.sum(jnp.where(rows == count - 1, total, 0.0), axis=0, keepdims=True)
                gap = jnp.exp(jnp.minimum(last - total, 0.0))
                key = recv[source, :, channels + at : channels + at + LANES].astype(F32)
                value = recv[source, :, 2 * channels + at : 2 * channels + at + LANES].astype(F32)
                spread(keys, c, jnp.where(rows < count, key * gap, 0.0), low, False)
                spread(values, c, value, low, True)
                spread(decays, c, jnp.broadcast_to(jnp.exp(last), (length, LANES)), low, False)
            for g in range(groups):
                key_of = [keys[token_rows(length, g, t), :] for t in range(length)]
                value_of = [values[token_rows(length, g, t), :] for t in range(length)]
                decay = decays[token_rows(length, g, 0), :]
                for tile in range(tiles):
                    at = slice(tile * LANES, (tile + 1) * LANES)
                    index = half + 2 * tile
                    state = take(decay, index) * store[row, g * 8 : g * 8 + 8, at]
                    for t in range(length):
                        state = state + take(key_of[t], index) * value_of[t]
                    out[row, g * 8 : g * 8 + 8, at] = state


def local_kernel(r, k, v, w, bonus, after, out):
    del after
    length = 8
    sessions = r.shape[0] // length
    columns = r.shape[1] // LANES
    low = lane_ids(length) < GROUP_WIDTH
    rows = row_ids(length)

    @pl.loop(0, sessions)
    def _(j):
        at = pl.ds(pl.multiple_of(j * length, length), length)
        for c in range(columns):
            cols = slice(c * LANES, (c + 1) * LANES)
            step, total = running_decay(w[at, cols])
            query = r[at, cols].astype(F32)
            key = k[at, cols].astype(F32)
            value = v[at, cols].astype(F32)
            wkv = half_sums(query * bonus[:, cols] * key, low) * value
            decayed = query * jnp.exp(total - step)
            grown = key * jnp.exp(-total)
            for back in range(1, length):
                score = half_sums(decayed * pltpu.roll(grown, back, 0), low)
                wkv = wkv + jnp.where(rows >= back, score * pltpu.roll(value, back, 0), 0.0)
            out[at, cols] = wkv


def finish_kernel(store_rows, hold, label, count, recv, part, gate, gain, shift, out):
    _, length, channels = recv.shape
    low = lane_ids(length) < GROUP_WIDTH
    rows = row_ids(length)
    for j in range(label.shape[0]):
        owner, _ = place_of(hold, label, j, store_rows)
        at = slice(j * length, (j + 1) * length)
        for c in range(channels // LANES):
            cols = slice(c * LANES, (c + 1) * LANES)
            wkv = recv[owner, :, cols] + part[at, cols]
            centred = wkv - half_sums(wkv, low) * (1.0 / GROUP_WIDTH)
            variance = half_sums(centred * centred, low) * (1.0 / GROUP_WIDTH)
            normed = centred * lax.rsqrt(variance + EPS) * gain[:, cols] + shift[:, cols]
            g = gate[at, cols].astype(F32)
            gated = normed * (g / (1.0 + jnp.exp(-g)))
            out[at, cols] = jnp.where(rows < count[j], gated, 0.0).astype(BF16)


def cost(flops, nbytes):
    return pl.CostEstimate(flops=flops, bytes_accessed=nbytes, transcendentals=0)


def shards(r, k, v, w, gate, bonus, gain, shift, store, hold, label, count):
    devices = lax.axis_size("cache")
    sessions = label.shape[0]
    store_rows, heads, state = store.shape
    tokens, channels = r.shape
    length = tokens // sessions
    width = 4 * channels + META
    send = pl.pallas_call(
        functools.partial(pack_kernel, store_rows),
        out_shape=jax.ShapeDtypeStruct((devices, length, width), BF16),
        in_specs=[SMEM()] * 3 + [VMEM()] * 4,
        out_specs=VMEM(),
        name="pack",
    )(hold, label, count, r, k, v, w)
    recv = lax.all_to_all(send, "cache", split_axis=0, concat_axis=0, tiled=True)
    part = pl.pallas_call(
        local_kernel,
        out_shape=jax.ShapeDtypeStruct((tokens, channels), F32),
        in_specs=[VMEM()] * 5 + [pl.BlockSpec(memory_space=pl.ANY)],
        out_specs=VMEM(),
        cost_estimate=cost(8_000_000, 400_000),
        name="local",
    )(r, k, v, w, bonus.reshape(1, channels), send)
    back = pl.pallas_call(
        state_read_kernel,
        out_shape=jax.ShapeDtypeStruct((devices, length, channels), F32),
        in_specs=[VMEM()] * 2,
        out_specs=VMEM(),
        scratch_shapes=[pltpu.VMEM((heads * length, LANES), F32)] * 2,
        name="state_read",
    )(recv, store)
    returned = lax.all_to_all(back, "cache", split_axis=0, concat_axis=0, tiled=True)
    updated = pl.pallas_call(
        state_write_kernel,
        out_shape=jax.ShapeDtypeStruct(store.shape, F32),
        in_specs=[VMEM(), pl.BlockSpec(memory_space=pl.ANY), VMEM()],
        out_specs=VMEM(),
        scratch_shapes=[pltpu.VMEM((heads * length, LANES), F32)] * 3,
        cost_estimate=cost(8_000_000, 3_000_000),
        name="state_write",
    )(recv, back, store)
    mixed = pl.pallas_call(
        functools.partial(finish_kernel, store_rows),
        out_shape=jax.ShapeDtypeStruct((tokens, channels), BF16),
        in_specs=[SMEM()] * 3 + [VMEM()] * 5,
        out_specs=VMEM(),
        name="finish",
    )(hold, label, count, returned, part, gate, gain.reshape(1, channels), shift.reshape(1, channels))
    return mixed, updated


def solution(mesh):
    rows = P(("groups", "cache"), "mp")
    states = P(("groups", "cache"), "mp", None)
    owned = P(("groups", "cache"))
    in_specs = (rows,) * 5 + (P("mp"),) * 3 + (states, P("groups"), owned, owned)
    return jax.shard_map(
        shards, mesh=mesh, in_specs=in_specs, out_specs=(rows, states), check_vma=False
    )
```

time: 106 us -> 50.2 us (0.47)
  the two profiles are of different devices: /device:TPU:0 before, /device:TPU:6 now
where the time goes in v1:
time: 50.2 us; the launch traced here: 49.7 us
  Pallas kernels  23.5 us (47%)
  blocking collectives  20.7 us (41%)
  starting transfers between devices  4.17 us (8%)
  local copies, waits for them, and re-layouts  0.69 us (1%)
  between operations  0.63 us (1%)
    all_to_all x1, blocking collectives, shards(): lax.all_to_all(send, 'cache', split_axis=0, concat_axis=0, tiled=True)  20.7 us
    pallas_call x1, Pallas kernels, shards(): pl.pallas_call(state_write_kernel, out_shape=jax.ShapeDtypeStruct(store.s...  8.77 us
    pallas_call x1, Pallas kernels, shards(): pl.pallas_call(state_read_kernel, out_shape=jax.ShapeDtypeStruct((devices...  8.46 us
    all_to_all x1, starting transfers between devices, shards(): lax.all_to_all(back, 'cache', split_axis=0, concat_axis=0, tiled=True)  4.17 us
    pallas_call x1, Pallas kernels, shards(): pl.pallas_call(local_kernel, out_shape=jax.ShapeDtypeStruct((tokens, chan...  2.55 us
    pallas_call x1, Pallas kernels, shards(): pl.pallas_call(functools.partial(finish_kernel, store_rows), out_shape=ja...  1.93 us
    pallas_call x1, Pallas kernels, shards(): pl.pallas_call(functools.partial(pack_kernel, store_rows), out_shape=jax....  1.78 us
  transfers between devices with their start and end apart: 1, of which 0 were waited for; matrix products, arithmetic and copies ran while one was open for 0% of the time, Pallas kernels for 23%

profile of v1, /device:TPU:6, one launch (start us, length us, event | category | flops | bytes accessed | tf_op | source)
XLA Modules:
  0.0 49.7 jit_solution(2970805297605767751)
XLA Ops:
  0.6 1.8 %pack.1.after = bf16[8,8,4224]{2,1,0:T(8,128)(2,1)} custom-call(s32[40]{0:T(128)} %hold.3, s32[4]{0:T(128)} %label.3, s32[4]{0:T(128)} %count.3, bf16[32,1024]{1,0:T(8,128)(2,1)} %r.3, bf16[32,1024]{1,0:T(8,128)(2,1)} %k.3, bf16[32,1024]{1,0:T(8,128)(2,1)} %v.3, bf16[32,1024]{1,0:T(8,128)(2,1)} %w.3), custom_call_target="tpu_custom_call" | custom-call | tf_op jit(solution)/shard_map/pack/pallas_call | solution.py:223
  2.4 20.7 %all_to_all.10.recv = bf16[8,8,4224]{2,1,0:T(8,128)(2,1)} all-to-all(bf16[8,8,4224]{2,1,0:T(8,128)(2,1)} %pack.1.after), channel_id=1, replica_groups=mesh['groups'=2,'cache'=8,'mp'=2] {'cache'}, dimensions={0} | all-to-all | bytes 1081344 | tf_op jit(solution)/shard_map/all_to_all | solution.py:230
  23.1 8.5 %state_read.1.after = f32[8,8,1024]{2,1,0:T(8,128)} custom-call(bf16[8,8,4224]{2,1,0:T(8,128)(2,1)} %all_to_all.10.recv, f32[5,16,4096]{2,1,0:T(8,128)} %store.3), custom_call_target="tpu_custom_call" | custom-call | tf_op jit(solution)/shard_map/state_read/pallas_call | solution.py:239
  31.6 4.2 %all-to-all-start.1 = ((f32[8,8,1024]{2,1,0:T(8,128)}), f32[8,8,1024]{2,1,0:T(8,128)S(1)}, u32[]{:S(2)}, u32[]{:S(2)}) async-start(f32[8,8,1024]{2,1,0:T(8,128)} %state_read.1.after), calls=%async_computation.1 | async-start | bytes 524288 | tf_op jit(solution)/shard_map/all_to_all | solution.py:247
  35.8 2.5 %local.1.part = f32[32,1024]{1,0:T(8,128)} custom-call(bf16[32,1024]{1,0:T(8,128)(2,1)} %r.3, bf16[32,1024]{1,0:T(8,128)(2,1)} %k.3, bf16[32,1024]{1,0:T(8,128)(2,1)} %v.3, bf16[32,1024]{1,0:T(8,128)(2,1)} %w.3, f32[1,1024]{1,0:T(1,128)} %bitcast.3, bf16[8,8,4224]{2,1,0:T(8,128)(2,1)} %pack.1.after), custom_call_target="tpu_custom_call" | custom-call | flops 8000000 | bytes 400000 | tf_op jit(solution)/shard_map/local/pallas_call | solution.py:231
  38.3 8.8 %state_write.1 = f32[5,16,4096]{2,1,0:T(8,128)} custom-call(bf16[8,8,4224]{2,1,0:T(8,128)(2,1)} %all_to_all.10.recv, f32[8,8,1024]{2,1,0:T(8,128)} %state_read.1.after, f32[5,16,4096]{2,1,0:T(8,128)} %store.3), custom_call_target="tpu_custom_call" | custom-call | flops 8000000 | bytes 3000000 | tf_op jit(solution)/shard_map/state_write/pallas_call | solution.py:248
  47.1 0.0 all-to-all-done.1.recv
  47.1 0.0 copy-start
  47.1 0.7 %copy-done = f32[8,8,1024]{2,1,0:T(8,128)} copy-done((f32[8,8,1024]{2,1,0:T(8,128)}, f32[8,8,1024]{2,1,0:T(8,128)S(1)}, u32[]{:S(2)}) %copy-start) | copy-done | bytes 262168
  47.8 1.9 %finish.1 = bf16[32,1024]{1,0:T(8,128)(2,1)} custom-call(s32[40]{0:T(128)} %hold.3, s32[4]{0:T(128)} %label.3, s32[4]{0:T(128)} %count.3, f32[8,8,1024]{2,1,0:T(8,128)} %copy-done, f32[32,1024]{1,0:T(8,128)} %local.1.part, bf16[32,1024]{1,0:T(8,128)(2,1)} %gate.1, f32[1,1024]{1,0:T(1,128)} %bitcast.4, f32[1,1024]{1,0:T(1,128)} %bitcast.5), custom_call_target="tpu_custom_call" | custom-call | tf_op jit(solution)/shard_map/finish/pallas_call | solution.py:257
Async XLA Ops:
  31.6 15.5 %all-to-all-start.1 = ((f32[8,8,1024]{2,1,0:T(8,128)}), f32[8,8,1024]{2,1,0:T(8,128)S(1)}, u32[]{:S(2)}, u32[]{:S(2)}) async-start(f32[8,8,1024]{2,1,0:T(8,128)} %state_read.1.after), calls=%async_computation.1 | async-start | bytes 524288 | tf_op jit(solution)/shard_map/all_to_all | solution.py:247
  47.1 0.7 %copy-start = (f32[8,8,1024]{2,1,0:T(8,128)}, f32[8,8,1024]{2,1,0:T(8,128)S(1)}, u32[]{:S(2)}) copy-start(f32[8,8,1024]{2,1,0:T(8,128)S(1)} %all-to-all-done.1.recv) | copy-start | bytes 786436

commit v2 on v1

--- a/solution.py
+++ b/solution.py
@@ -11,6 +11,7 @@
 EPS = 0.00064
 LANES = 128
 META = 128
+UNROLL = 4
 F32 = jnp.float32
 BF16 = jnp.bfloat16
 
@@ -49,7 +50,7 @@
     return jnp.where(low, first, second)
 
 
-def pack_kernel(store_rows, hold, label, count, r, k, v, w, out):
+def pack_kernel(store_rows, hold, label, count, r, k, v, w, out, route):
     devices, length, _ = out.shape
     channels = r.shape[1]
     lanes = lane_ids(length)
@@ -57,6 +58,8 @@
         out[d, :, 4 * channels :] = jnp.zeros((length, META), BF16)
     for j in range(label.shape[0]):
         owner, local = place_of(hold, label, j, store_rows)
+        route[2 * j] = owner
+        route[2 * j + 1] = count[j]
         rows = pl.ds(j * length, length)
         for index, ref in enumerate((r, k, v, w)):
             out[owner, :, index * channels : (index + 1) * channels] = ref[rows, :]
@@ -64,11 +67,13 @@
         out[owner, :, 4 * channels :] = meta.astype(F32).astype(BF16)
 
 
-def meta_of(recv, source, base):
-    tile = recv[source, :, base:].astype(F32)
-    lanes = lane_ids(tile.shape[0])
-    row = jnp.max(jnp.where(lanes == 0, tile, 0.0)).astype(jnp.int32) - 1
-    return row, jnp.max(jnp.where(lanes == 1, tile, 0.0)).astype(jnp.int32)
+def read_meta(recv, base, table):
+    for source in range(recv.shape[0]):
+        tile = recv[source, :, base:].astype(F32)
+        lanes = lane_ids(tile.shape[0])
+        tile = jnp.where(lanes == 0, 16.0 * tile, jnp.where(lanes == 1, tile, 0.0))
+        first = jnp.sum(jnp.where(row_ids(tile.shape[0]) == 0, tile, 0.0))
+        table[source] = first.astype(jnp.int32)
 
 
 def spread(scratch, column, tile, low, both):
@@ -88,18 +93,19 @@
     return jnp.take_along_axis(x, index, axis=1, mode="promise_in_bounds")
 
 
-def state_read_kernel(recv, store, out, scratch, result):
+def state_read_kernel(recv, store, part, out, table, scratch, result):
+    del part
     devices, length, channels = out.shape
     columns = channels // LANES
     groups = store.shape[1] // 8
     tiles = store.shape[2] // LANES
     low = lane_ids(length) < GROUP_WIDTH
-    low8 = lane_ids(8) < GROUP_WIDTH
-    half = jnp.where(low8, 0, 1)
+    half = jnp.where(lane_ids(8) < GROUP_WIDTH, 0, 1)
+    read_meta(recv, 4 * channels, table)
 
     @pl.loop(0, devices)
     def _(source):
-        row, _ = meta_of(recv, source, 4 * channels)
+        row = lax.div(table[source], 16) - 1
 
         @pl.when(row >= 0)
         def _():
@@ -108,23 +114,32 @@
                 step, total = running_decay(recv[source, :, 3 * channels + at : 3 * channels + at + LANES])
                 decayed = recv[source, :, at : at + LANES].astype(F32) * jnp.exp(total - step)
                 spread(scratch, c, decayed, low, False)
+            queries = [
+                [scratch[token_rows(length, g, t), :] for t in range(length)] for g in range(groups)
+            ]
+
+            def accumulate(tile, sums):
+                at = pl.ds(pl.multiple_of(tile * LANES, LANES), LANES)
+                index = half + 2 * tile
+                states = [store[row, g * 8 : g * 8 + 8, at] for g in range(groups)]
+                return tuple(
+                    tuple(sums[g][t] + take(queries[g][t], index) * states[g] for t in range(length))
+                    for g in range(groups)
+                )
+
+            zero = jnp.zeros((8, LANES), F32)
+            sums = lax.fori_loop(0, tiles, accumulate, ((zero,) * length,) * groups, unroll=UNROLL)
             for g in range(groups):
-                queries = [scratch[token_rows(length, g, t), :] for t in range(length)]
-                sums = [jnp.zeros((8, LANES), F32) for _ in range(length)]
-                for tile in range(tiles):
-                    state = store[row, g * 8 : g * 8 + 8, tile * LANES : (tile + 1) * LANES]
-                    index = half + 2 * tile
-                    for t in range(length):
-                        sums[t] = sums[t] + take(queries[t], index) * state
                 for t in range(length):
-                    result[token_rows(length, g, t), :] = sums[t] + pltpu.roll(sums[t], GROUP_WIDTH, 1)
+                    total = sums[g][t]
+                    result[token_rows(length, g, t), :] = total + pltpu.roll(total, GROUP_WIDTH, 1)
             for c in range(columns):
                 even = result[2 * c * length : (2 * c + 1) * length, :]
                 odd = result[(2 * c + 1) * length : (2 * c + 2) * length, :]
                 out[source, :, c * LANES : (c + 1) * LANES] = jnp.where(low, even, odd)
 
 
-def state_write_kernel(recv, after, store, out, keys, values, decays):
+def state_write_kernel(table, recv, after, store, out, keys, values, decays):
     del after
     devices, length, width = recv.shape
     channels = (width - META) // 4
@@ -138,7 +153,8 @@
 
     @pl.loop(0, devices)
     def _(source):
-        row, count = meta_of(recv, source, 4 * channels)
+        row = lax.div(table[source], 16) - 1
+        count = lax.rem(table[source], 16)
 
         @pl.when(row >= 0)
         def _():
@@ -152,16 +168,19 @@
                 spread(keys, c, jnp.where(rows < count, key * gap, 0.0), low, False)
                 spread(values, c, value, low, True)
                 spread(decays, c, jnp.broadcast_to(jnp.exp(last), (length, LANES)), low, False)
-            for g in range(groups):
-                key_of = [keys[token_rows(length, g, t), :] for t in range(length)]
-                value_of = [values[token_rows(length, g, t), :] for t in range(length)]
-                decay = decays[token_rows(length, g, 0), :]
-                for tile in range(tiles):
-                    at = slice(tile * LANES, (tile + 1) * LANES)
-                    index = half + 2 * tile
-                    state = take(decay, index) * store[row, g * 8 : g * 8 + 8, at]
-                    for t in range(length):
-                        state = state + take(key_of[t], index) * value_of[t]
+            span = range(length)
+            key_of = [[keys[token_rows(length, g, t), :] for t in span] for g in range(groups)]
+            value_of = [[values[token_rows(length, g, t), :] for t in span] for g in range(groups)]
+            decay = [decays[token_rows(length, g, 0), :] for g in range(groups)]
+
+            @pl.loop(0, tiles, unroll=UNROLL)
+            def _(tile):
+                at = pl.ds(pl.multiple_of(tile * LANES, LANES), LANES)
+                index = half + 2 * tile
+                for g in range(groups):
+                    state = take(decay[g], index) * store[row, g * 8 : g * 8 + 8, at]
+                    for t in span:
+                        state = state + take(key_of[g][t], index) * value_of[g][t]
                     out[row, g * 8 : g * 8 + 8, at] = state
 
 
@@ -191,12 +210,12 @@
             out[at, cols] = wkv
 
 
-def finish_kernel(store_rows, hold, label, count, recv, part, gate, gain, shift, out):
+def finish_kernel(route, recv, part, gate, gain, shift, out):
     _, length, channels = recv.shape
     low = lane_ids(length) < GROUP_WIDTH
     rows = row_ids(length)
-    for j in range(label.shape[0]):
-        owner, _ = place_of(hold, label, j, store_rows)
+    for j in range(out.shape[0] // length):
+        owner, count = route[2 * j], route[2 * j + 1]
         at = slice(j * length, (j + 1) * length)
         for c in range(channels // LANES):
             cols = slice(c * LANES, (c + 1) * LANES)
@@ -206,11 +225,22 @@
             normed = centred * lax.rsqrt(variance + EPS) * gain[:, cols] + shift[:, cols]
             g = gate[at, cols].astype(F32)
             gated = normed * (g / (1.0 + jnp.exp(-g)))
-            out[at, cols] = jnp.where(rows < count[j], gated, 0.0).astype(BF16)
+            out[at, cols] = jnp.where(rows < count, gated, 0.0).astype(BF16)
 
 
 def cost(flops, nbytes):
     return pl.CostEstimate(flops=flops, bytes_accessed=nbytes, transcendentals=0)
+
+
+PARAMS = pltpu.CompilerParams(vmem_limit_bytes=24 * 2**20)
+
+
+def in_vmem(x):
+    return pltpu.with_memory_space_constraint(x, pltpu.VMEM)
+
+
+def in_smem(x):
+    return pltpu.with_memory_space_constraint(x, pltpu.SMEM)
 
 
 def shards(r, k, v, w, gate, bonus, gain, shift, store, hold, label, count):
@@ -220,47 +250,59 @@
     tokens, channels = r.shape
     length = tokens // sessions
     width = 4 * channels + META
-    send = pl.pallas_call(
+    send, route = pl.pallas_call(
         functools.partial(pack_kernel, store_rows),
-        out_shape=jax.ShapeDtypeStruct((devices, length, width), BF16),
+        out_shape=(
+            jax.ShapeDtypeStruct((devices, length, width), BF16),
+            pltpu.SMEM((2 * sessions,), jnp.int32),
+        ),
         in_specs=[SMEM()] * 3 + [VMEM()] * 4,
-        out_specs=VMEM(),
+        out_specs=(VMEM(), SMEM()),
+        compiler_params=PARAMS,
         name="pack",
     )(hold, label, count, r, k, v, w)
-    recv = lax.all_to_all(send, "cache", split_axis=0, concat_axis=0, tiled=True)
+    recv = in_vmem(lax.all_to_all(send, "cache", split_axis=0, concat_axis=0, tiled=True))
     part = pl.pallas_call(
         local_kernel,
-        out_shape=jax.ShapeDtypeStruct((tokens, channels), F32),
+        out_shape=pltpu.VMEM((tokens, channels), F32),
         in_specs=[VMEM()] * 5 + [pl.BlockSpec(memory_space=pl.ANY)],
         out_specs=VMEM(),
         cost_estimate=cost(8_000_000, 400_000),
+        compiler_params=PARAMS,
         name="local",
     )(r, k, v, w, bonus.reshape(1, channels), send)
-    back = pl.pallas_call(
+    resident = in_vmem(store)
+    back, table = pl.pallas_call(
         state_read_kernel,
-        out_shape=jax.ShapeDtypeStruct((devices, length, channels), F32),
-        in_specs=[VMEM()] * 2,
-        out_specs=VMEM(),
+        out_shape=(
+            jax.ShapeDtypeStruct((devices, length, channels), F32),
+            pltpu.SMEM((devices,), jnp.int32),
+        ),
+        in_specs=[VMEM()] * 3,
+        out_specs=(VMEM(), SMEM()),
         scratch_shapes=[pltpu.VMEM((heads * length, LANES), F32)] * 2,
+        compiler_params=PARAMS,
         name="state_read",
-    )(recv, store)
-    returned = lax.all_to_all(back, "cache", split_axis=0, concat_axis=0, tiled=True)
+    )(recv, resident, in_vmem(part))
+    returned = in_vmem(lax.all_to_all(back, "cache", split_axis=0, concat_axis=0, tiled=True))
     updated = pl.pallas_call(
         state_write_kernel,
         out_shape=jax.ShapeDtypeStruct(store.shape, F32),
-        in_specs=[VMEM(), pl.BlockSpec(memory_space=pl.ANY), VMEM()],
+        in_specs=[SMEM(), VMEM(), pl.BlockSpec(memory_space=pl.ANY), VMEM()],
         out_specs=VMEM(),
         scratch_shapes=[pltpu.VMEM((heads * length, LANES), F32)] * 3,
         cost_estimate=cost(8_000_000, 3_000_000),
+        compiler_params=PARAMS,
         name="state_write",
-    )(recv, back, store)
+    )(in_smem(table), recv, back, resident)
     mixed = pl.pallas_call(
-        functools.partial(finish_kernel, store_rows),
+        finish_kernel,
         out_shape=jax.ShapeDtypeStruct((tokens, channels), BF16),
-        in_specs=[SMEM()] * 3 + [VMEM()] * 5,
+        in_specs=[SMEM()] + [VMEM()] * 5,
         out_specs=VMEM(),
+        compiler_params=PARAMS,
         name="finish",
-    )(hold, label, count, returned, part, gate, gain.reshape(1, channels), shift.reshape(1, channels))
+    )(in_smem(route), returned, in_vmem(part), in_vmem(gate), gain.reshape(1, channels), shift.reshape(1, channels))
     return mixed, updated
 
 

time: 50.2 us -> 50.6 us (level)
  the two profiles are of different devices: /device:TPU:6 before, /device:TPU:0 now
where the time goes in v2:
time: 50.6 us; the launch traced here: 50.3 us
  Pallas kernels  19.6 us (39%)
  starting transfers between devices  10.7 us (21%)
  waiting for transfers between devices  10.5 us (21%)
  local copies, waits for them, and re-layouts  8.8 us (17%)
  between operations  0.72 us (1%)
    all_to_all x1, waiting for transfers between devices, shards(): lax.all_to_all(send, 'cache', split_axis=0, concat_axis=0, tiled=True)  10.5 us
    unnamed x32, local copies, waits for them, and re-layouts  8.8 us
    pallas_call x1, Pallas kernels, shards(): pl.pallas_call(state_write_kernel, out_shape=jax.ShapeDtypeStruct(store.s...  8.48 us
    pallas_call x1, Pallas kernels, shards(): pl.pallas_call(state_read_kernel, out_shape=(jax.ShapeDtypeStruct((device...  7.87 us
    all_to_all x1, starting transfers between devices, shards(): lax.all_to_all(send, 'cache', split_axis=0, concat_axis=0, tiled=True)  7.31 us
    all_to_all x1, starting transfers between devices, shards(): lax.all_to_all(back, 'cache', split_axis=0, concat_axis=0, tiled=True)  3.41 us
    pallas_call x1, Pallas kernels, shards(): pl.pallas_call(functools.partial(pack_kernel, store_rows), out_shape=(jax...  1.38 us
  transfers between devices with their start and end apart: 2, of which 1 were waited for; matrix products, arithmetic and copies ran while one was open for 0% of the time, Pallas kernels for 19%

profile of v2, /device:TPU:0, one launch (start us, length us, event | category | flops | bytes accessed | tf_op | source)
XLA Modules:
  0.0 50.3 jit_solution(411019718917658987)
XLA Ops:
  0.6 0.0 copy-start.1
  0.7 0.9 %copy-done.1 = bf16[32,1024]{1,0:T(8,128)(2,1)S(1)} copy-done((bf16[32,1024]{1,0:T(8,128)(2,1)S(1)}, bf16[32,1024]{1,0:T(8,128)(2,1)}, u32[]{:S(2)}) %copy-start.1) | copy-done | bytes 65560
  1.6 0.8 %copy-done.3 = bf16[32,1024]{1,0:T(8,128)(2,1)S(1)} copy-done((bf16[32,1024]{1,0:T(8,128)(2,1)S(1)}, bf16[32,1024]{1,0:T(8,128)(2,1)}, u32[]{:S(2)}) %copy-start.3) | copy-done | bytes 65560
  2.4 0.8 %copy-done.5 = bf16[32,1024]{1,0:T(8,128)(2,1)S(1)} copy-done((bf16[32,1024]{1,0:T(8,128)(2,1)S(1)}, bf16[32,1024]{1,0:T(8,128)(2,1)}, u32[]{:S(2)}) %copy-start.5) | copy-done | bytes 65560
  3.3 0.8 %copy-done.7 = bf16[32,1024]{1,0:T(8,128)(2,1)S(1)} copy-done((bf16[32,1024]{1,0:T(8,128)(2,1)S(1)}, bf16[32,1024]{1,0:T(8,128)(2,1)}, u32[]{:S(2)}) %copy-start.7) | copy-done | bytes 65560
  4.1 0.7 %copy-done.13 = s32[40]{0:T(128)S(1)} copy-done((s32[40]{0:T(128)S(1)}, s32[40]{0:T(128)}, u32[]{:S(2)}) %copy-start.13) | copy-done | bytes 184
  4.8 0.7 %copy-done.14 = s32[4]{0:T(128)S(1)} copy-done((s32[4]{0:T(128)S(1)}, s32[4]{0:T(128)}, u32[]{:S(2)}) %copy-start.14) | copy-done | bytes 40
  5.4 0.7 %copy-done.15 = s32[4]{0:T(128)S(1)} copy-done((s32[4]{0:T(128)S(1)}, s32[4]{0:T(128)}, u32[]{:S(2)}) %copy-start.15) | copy-done | bytes 40
  6.1 1.4 %pack.1 = (bf16[8,8,4224]{2,1,0:T(8,128)(2,1)}, s32[8]{0:T(128)S(4)}) custom-call(s32[40]{0:T(128)S(1)} %copy-done.13, s32[4]{0:T(128)S(1)} %copy-done.14, s32[4]{0:T(128)S(1)} %copy-done.15, bf16[32,1024]{1,0:T(8,128)(2,1)S(1)} %copy-done.1, bf16[32,1024]{1,0:T(8,128)(2,1)S(1)} %copy-done.3, bf16[32,1024]{1,0:T(8,128)(2,1)S(1)} %copy-done.5, ...), custom_call_target="tpu_custom_call" | custom-call | tf_op jit(solution)/shard_map/pack/pallas_call | solution.py:253
  7.5 7.3 %all-to-all-start = ((bf16[8,8,4224]{2,1,0:T(8,128)(2,1)}), bf16[8,8,4224]{2,1,0:T(8,128)(2,1)S(1)}, u32[]{:S(2)}, u32[]{:S(2)}) async-start(bf16[8,8,4224]{2,1,0:T(8,128)(2,1)} %get-tuple-element.7.after), calls=%async_computation | async-start | bytes 1081344 | tf_op jit(solution)/shard_map/all_to_all | solution.py:264
  14.8 0.0 copy-start.2
  14.8 0.8 %copy-done.2 = bf16[32,1024]{1,0:T(8,128)(2,1)S(1)} copy-done((bf16[32,1024]{1,0:T(8,128)(2,1)S(1)}, bf16[32,1024]{1,0:T(8,128)(2,1)}, u32[]{:S(2)}) %copy-start.2) | copy-done | bytes 65560
  15.6 0.8 %copy-done.4 = bf16[32,1024]{1,0:T(8,128)(2,1)S(1)} copy-done((bf16[32,1024]{1,0:T(8,128)(2,1)S(1)}, bf16[32,1024]{1,0:T(8,128)(2,1)}, u32[]{:S(2)}) %copy-start.4) | copy-done | bytes 65560
  16.5 0.8 %copy-done.6 = bf16[32,1024]{1,0:T(8,128)(2,1)S(1)} copy-done((bf16[32,1024]{1,0:T(8,128)(2,1)S(1)}, bf16[32,1024]{1,0:T(8,128)(2,1)}, u32[]{:S(2)}) %copy-start.6) | copy-done | bytes 65560
  17.3 0.8 %copy-done.8 = bf16[32,1024]{1,0:T(8,128)(2,1)S(1)} copy-done((bf16[32,1024]{1,0:T(8,128)(2,1)S(1)}, bf16[32,1024]{1,0:T(8,128)(2,1)}, u32[]{:S(2)}) %copy-start.8) | copy-done | bytes 65560
  18.1 1.0 %local.1.part = f32[32,1024]{1,0:T(8,128)S(1)} custom-call(bf16[32,1024]{1,0:T(8,128)(2,1)S(1)} %copy-done.2, bf16[32,1024]{1,0:T(8,128)(2,1)S(1)} %copy-done.4, bf16[32,1024]{1,0:T(8,128)(2,1)S(1)} %copy-done.6, bf16[32,1024]{1,0:T(8,128)(2,1)S(1)} %copy-done.8, f32[1,1024]{1,0:T(1,128)S(1)} %bitcast.3, bf16[8,8,4224]{2,1,0:T(8,128)(2,1)} %get-tuple-element.7.after), custom_call_target="tpu_custom_call" | custom-call | flops 8000000 | bytes 400000 | tf_op jit(solution)/shard_map/local/pallas_call | solution.py:265
  19.1 10.5 %all-to-all-done.recv = bf16[8,8,4224]{2,1,0:T(8,128)(2,1)S(1)} async-done(((bf16[8,8,4224]{2,1,0:T(8,128)(2,1)}), bf16[8,8,4224]{2,1,0:T(8,128)(2,1)S(1)}, u32[]{:S(2)}, u32[]{:S(2)}) %all-to-all-start) | async-done | bytes 540704 | tf_op jit(solution)/shard_map/all_to_all | solution.py:264
  29.6 7.9 %state_read.1 = (f32[8,8,1024]{2,1,0:T(8,128)}, s32[8]{0:T(128)S(4)}) custom-call(bf16[8,8,4224]{2,1,0:T(8,128)(2,1)S(1)} %all-to-all-done.recv, f32[5,16,4096]{2,1,0:T(8,128)S(1)} %copy-done, f32[32,1024]{1,0:T(8,128)S(1)} %local.1.part), custom_call_target="tpu_custom_call" | custom-call | tf_op jit(solution)/shard_map/state_read/pallas_call | solution.py:275
  37.5 3.4 %all-to-all-start.1 = ((f32[8,8,1024]{2,1,0:T(8,128)}), f32[8,8,1024]{2,1,0:T(8,128)S(1)}, u32[]{:S(2)}, u32[]{:S(2)}) async-start(f32[8,8,1024]{2,1,0:T(8,128)} %get-tuple-element.8.after), calls=%async_computation.1 | async-start | bytes 524288 | tf_op jit(solution)/shard_map/all_to_all | solution.py:287
  40.9 0.0 copy-start.9
  40.9 0.0 copy-start.11
  40.9 0.0 copy-start.12
  40.9 8.5 %state_write.1 = f32[5,16,4096]{2,1,0:T(8,128)} custom-call(s32[8]{0:T(128)S(4)} %get-tuple-element.9.table, bf16[8,8,4224]{2,1,0:T(8,128)(2,1)S(1)} %all-to-all-done.recv, f32[8,8,1024]{2,1,0:T(8,128)} %get-tuple-element.8.after, f32[5,16,4096]{2,1,0:T(8,128)S(1)} %copy-done), custom_call_target="tpu_custom_call" | custom-call | flops 8000000 | bytes 3000000 | tf_op jit(solution)/shard_map/state_write/pallas_call | solution.py:288
  49.4 0.9 %finish.1 = bf16[32,1024]{1,0:T(8,128)(2,1)} custom-call(s32[8]{0:T(128)S(4)} %get-tuple-element.6.route, f32[8,8,1024]{2,1,0:T(8,128)S(1)} %all-to-all-done.1.recv, f32[32,1024]{1,0:T(8,128)S(1)} %local.1.part, bf16[32,1024]{1,0:T(8,128)(2,1)S(1)} %copy-done.9, f32[1,1024]{1,0:T(1,128)S(1)} %bitcast.4, f32[1,1024]{1,0:T(1,128)S(1)} %bitcast.5), custom_call_target="tpu_custom_call" | custom-call | tf_op jit(solution)/shard_map/finish/pallas_call | solution.py:298
  (17 shorter events, 0.0 us)
Async XLA Ops:
  0.6 29.0 %copy-start = (f32[5,16,4096]{2,1,0:T(8,128)S(1)}, f32[5,16,4096]{2,1,0:T(8,128)}, u32[]{:S(2)}) copy-start(f32[5,16,4096]{2,1,0:T(8,128)} %store.3) | copy-start | bytes 3932164
  0.6 0.9 %copy-start.1 = (bf16[32,1024]{1,0:T(8,128)(2,1)S(1)}, bf16[32,1024]{1,0:T(8,128)(2,1)}, u32[]{:S(2)}) copy-start(bf16[32,1024]{1,0:T(8,128)(2,1)} %r.3) | copy-start | bytes 196612
  1.6 0.8 %copy-start.3 = (bf16[32,1024]{1,0:T(8,128)(2,1)S(1)}, bf16[32,1024]{1,0:T(8,128)(2,1)}, u32[]{:S(2)}) copy-start(bf16[32,1024]{1,0:T(8,128)(2,1)} %k.3) | copy-start | bytes 196612
  2.4 0.8 %copy-start.5 = (bf16[32,1024]{1,0:T(8,128)(2,1)S(1)}, bf16[32,1024]{1,0:T(8,128)(2,1)}, u32[]{:S(2)}) copy-start(bf16[32,1024]{1,0:T(8,128)(2,1)} %v.3) | copy-start | bytes 196612
  3.3 0.8 %copy-start.7 = (bf16[32,1024]{1,0:T(8,128)(2,1)S(1)}, bf16[32,1024]{1,0:T(8,128)(2,1)}, u32[]{:S(2)}) copy-start(bf16[32,1024]{1,0:T(8,128)(2,1)} %w.3) | copy-start | bytes 196612
  4.1 0.7 %copy-start.13 = (s32[40]{0:T(128)S(1)}, s32[40]{0:T(128)}, u32[]{:S(2)}) copy-start(s32[40]{0:T(128)} %hold.1) | copy-start | bytes 484
  4.8 0.7 %copy-start.14 = (s32[4]{0:T(128)S(1)}, s32[4]{0:T(128)}, u32[]{:S(2)}) copy-start(s32[4]{0:T(128)} %label.1) | copy-start | bytes 52
  5.4 0.7 %copy-start.15 = (s32[4]{0:T(128)S(1)}, s32[4]{0:T(128)}, u32[]{:S(2)}) copy-start(s32[4]{0:T(128)} %count.1) | copy-start | bytes 52
  6.1 8.7 %copy-start.10 = (f32[1024]{0:T(1024)S(1)}, f32[1024]{0:T(1024)}, u32[]{:S(2)}) copy-start(f32[1024]{0:T(1024)} %param.17) | copy-start | bytes 12292
  7.5 22.1 %all-to-all-start = ((bf16[8,8,4224]{2,1,0:T(8,128)(2,1)}), bf16[8,8,4224]{2,1,0:T(8,128)(2,1)S(1)}, u32[]{:S(2)}, u32[]{:S(2)}) async-start(bf16[8,8,4224]{2,1,0:T(8,128)(2,1)} %get-tuple-element.7.after), calls=%async_computation | async-start | bytes 1081344 | tf_op jit(solution)/shard_map/all_to_all | solution.py:264
  14.8 0.8 %copy-start.2 = (bf16[32,1024]{1,0:T(8,128)(2,1)S(1)}, bf16[32,1024]{1,0:T(8,128)(2,1)}, u32[]{:S(2)}) copy-start(bf16[32,1024]{1,0:T(8,128)(2,1)} %r.3) | copy-start | bytes 196612
  15.6 0.8 %copy-start.4 = (bf16[32,1024]{1,0:T(8,128)(2,1)S(1)}, bf16[32,1024]{1,0:T(8,128)(2,1)}, u32[]{:S(2)}) copy-start(bf16[32,1024]{1,0:T(8,128)(2,1)} %k.3) | copy-start | bytes 196612
  16.5 0.8 %copy-start.6 = (bf16[32,1024]{1,0:T(8,128)(2,1)S(1)}, bf16[32,1024]{1,0:T(8,128)(2,1)}, u32[]{:S(2)}) copy-start(bf16[32,1024]{1,0:T(8,128)(2,1)} %v.3) | copy-start | bytes 196612
  17.3 0.8 %copy-start.8 = (bf16[32,1024]{1,0:T(8,128)(2,1)S(1)}, bf16[32,1024]{1,0:T(8,128)(2,1)}, u32[]{:S(2)}) copy-start(bf16[32,1024]{1,0:T(8,128)(2,1)} %w.3) | copy-start | bytes 196612
  37.5 11.9 %all-to-all-start.1 = ((f32[8,8,1024]{2,1,0:T(8,128)}), f32[8,8,1024]{2,1,0:T(8,128)S(1)}, u32[]{:S(2)}, u32[]{:S(2)}) async-start(f32[8,8,1024]{2,1,0:T(8,128)} %get-tuple-element.8.after), calls=%async_computation.1 | async-start | bytes 524288 | tf_op jit(solution)/shard_map/all_to_all | solution.py:287
  40.9 8.5 %copy-start.9 = (bf16[32,1024]{1,0:T(8,128)(2,1)S(1)}, bf16[32,1024]{1,0:T(8,128)(2,1)}, u32[]{:S(2)}) copy-start(bf16[32,1024]{1,0:T(8,128)(2,1)} %gate.1) | copy-start | bytes 196612
  40.9 8.5 %copy-start.11 = (f32[1024]{0:T(1024)S(1)}, f32[1024]{0:T(1024)}, u32[]{:S(2)}) copy-start(f32[1024]{0:T(1024)} %param.18) | copy-start | bytes 12292
  40.9 8.5 %copy-start.12 = (f32[1024]{0:T(1024)S(1)}, f32[1024]{0:T(1024)}, u32[]{:S(2)}) copy-start(f32[1024]{0:T(1024)} %param.19) | copy-start | bytes 12292

commit v3 on v2

--- a/solution.py
+++ b/solution.py
@@ -50,21 +50,50 @@
     return jnp.where(low, first, second)
 
 
-def pack_kernel(store_rows, hold, label, count, r, k, v, w, out, route):
+def pack_kernel(store_rows, *refs):
+    hold, label, count, *tensors = refs[:7]
+    out, route, hold_in, label_in, count_in, meta, loaded, sems, sent = refs[7:]
     devices, length, _ = out.shape
-    channels = r.shape[1]
+    channels = tensors[0].shape[1]
+    small = ((hold, hold_in), (label, label_in), (count, count_in))
+    large = tuple((ref, loaded.at[index]) for index, ref in enumerate(tensors))
+    loads = [
+        pltpu.make_async_copy(source, target, sems.at[index])
+        for index, (source, target) in enumerate(small + large)
+    ]
+    for load in loads:
+        load.start()
+    meta[...] = jnp.zeros(meta.shape, BF16)
+    for load in loads[: len(small)]:
+        load.wait()
     lanes = lane_ids(length)
-    for d in range(devices):
-        out[d, :, 4 * channels :] = jnp.zeros((length, META), BF16)
-    for j in range(label.shape[0]):
-        owner, local = place_of(hold, label, j, store_rows)
+    owners = []
+    for j in range(label_in.shape[0]):
+        owner, local = place_of(hold_in, label_in, j, store_rows)
+        owners.append(owner)
         route[2 * j] = owner
-        route[2 * j + 1] = count[j]
-        rows = pl.ds(j * length, length)
-        for index, ref in enumerate((r, k, v, w)):
-            out[owner, :, index * channels : (index + 1) * channels] = ref[rows, :]
-        meta = jnp.where(lanes == 0, local + 1, jnp.where(lanes == 1, count[j], 0))
-        out[owner, :, 4 * channels :] = meta.astype(F32).astype(BF16)
+        route[2 * j + 1] = count_in[j]
+        tile = jnp.where(lanes == 0, local + 1, jnp.where(lanes == 1, count_in[j], 0))
+        meta[owner] = tile.astype(F32).astype(BF16)
+    sends = []
+    for load in loads[len(small) :]:
+        load.wait()
+    for j, owner in enumerate(owners):
+        for index in range(len(tensors)):
+            sends.append(
+                pltpu.make_async_copy(
+                    loaded.at[index, j * length : (j + 1) * length],
+                    out.at[owner, :, index * channels : (index + 1) * channels],
+                    sent.at[len(sends)],
+                )
+            )
+            sends[-1].start()
+    sends.append(
+        pltpu.make_async_copy(meta, out.at[:, :, len(tensors) * channels :], sent.at[len(sends)])
+    )
+    sends[-1].start()
+    for send in sends:
+        send.wait()
 
 
 def read_meta(recv, base, table):
@@ -93,50 +122,99 @@
     return jnp.take_along_axis(x, index, axis=1, mode="promise_in_bounds")
 
 
-def state_read_kernel(recv, store, part, out, table, scratch, result):
+def split(x):
+    high = x.astype(BF16)
+    return high, (x - high.astype(F32)).astype(BF16)
+
+
+def retile_kernel(store, part, out, scratch):
     del part
+    tiles = store.shape[2] // LANES
+
+    @pl.loop(0, store.shape[0])
+    def _(row):
+        for g in range(store.shape[1] // 8):
+            for tile in range(tiles):
+                scratch[g, tile * 8 : tile * 8 + 8, :] = store[
+                    row, g * 8 : g * 8 + 8, tile * LANES : (tile + 1) * LANES
+                ]
+            for head in range(8):
+                for tile in range(0, tiles, 16):
+                    halves = [
+                        scratch[g, pl.ds(head + 8 * (tile + more), 8, stride=8), :] for more in (0, 8)
+                    ]
+                    high, low = split(jnp.concatenate(halves, axis=0))
+                    at = slice(head * tiles + tile, head * tiles + tile + 16)
+                    out[row, g, at, :LANES] = high
+                    out[row, g, at, LANES:] = low
+
+
+def state_read_kernel(recv, matrices, out, table, order, queries):
     devices, length, channels = out.shape
     columns = channels // LANES
-    groups = store.shape[1] // 8
-    tiles = store.shape[2] // LANES
-    low = lane_ids(length) < GROUP_WIDTH
-    half = jnp.where(lane_ids(8) < GROUP_WIDTH, 0, 1)
+    _, groups, depth, _ = matrices.shape
+    tiles = depth // 8
+    per_group = columns // groups
+    half_rows = 8 * 2 * length
+    lanes = lane_ids(length)
+    low = lanes < GROUP_WIDTH
+    spot = lanes % tiles
+    deal = (lanes // GROUP_WIDTH) * GROUP_WIDTH + 2 * spot + (lanes % GROUP_WIDTH) // tiles
+    queries[...] = jnp.zeros(queries.shape, BF16)
     read_meta(recv, 4 * channels, table)
 
-    @pl.loop(0, devices)
-    def _(source):
-        row = lax.div(table[source], 16) - 1
-
-        @pl.when(row >= 0)
-        def _():
-            for c in range(columns):
-                at = c * LANES
-                step, total = running_decay(recv[source, :, 3 * channels + at : 3 * channels + at + LANES])
-                decayed = recv[source, :, at : at + LANES].astype(F32) * jnp.exp(total - step)
-                spread(scratch, c, decayed, low, False)
-            queries = [
-                [scratch[token_rows(length, g, t), :] for t in range(length)] for g in range(groups)
-            ]
-
-            def accumulate(tile, sums):
-                at = pl.ds(pl.multiple_of(tile * LANES, LANES), LANES)
-                index = half + 2 * tile
-                states = [store[row, g * 8 : g * 8 + 8, at] for g in range(groups)]
-                return tuple(
-                    tuple(sums[g][t] + take(queries[g][t], index) * states[g] for t in range(length))
-                    for g in range(groups)
-                )
-
-            zero = jnp.zeros((8, LANES), F32)
-            sums = lax.fori_loop(0, tiles, accumulate, ((zero,) * length,) * groups, unroll=UNROLL)
-            for g in range(groups):
-                for t in range(length):
-                    total = sums[g][t]
-                    result[token_rows(length, g, t), :] = total + pltpu.roll(total, GROUP_WIDTH, 1)
-            for c in range(columns):
-                even = result[2 * c * length : (2 * c + 1) * length, :]
-                odd = result[(2 * c + 1) * length : (2 * c + 2) * length, :]
-                out[source, :, c * LANES : (c + 1) * LANES] = jnp.where(low, even, odd)
+    served = jnp.int32(0)
+    for source in range(devices):
+        served = served + jnp.where(table[source] > 0, 1, 0)
+    first, other = jnp.int32(0), served
+    for source in range(devices):
+        here = table[source] > 0
+        order[jnp.where(here, first, other)] = jnp.int32(source)
+        first = first + jnp.where(here, 1, 0)
+        other = other + jnp.where(here, 0, 1)
+
+    def lay_out(source):
+        for c in range(columns):
+            at = c * LANES
+            step, total = running_decay(recv[source, :, 3 * channels + at : 3 * channels + at + LANES])
+            decayed = recv[source, :, at : at + LANES].astype(F32) * jnp.exp(total - step)
+            dealt = take(decayed, deal)
+            for parity in range(2):
+                head = 2 * (c % per_group) + parity
+                quarter, side = head % 4, head // 4
+                blocks = []
+                for p in range(2):
+                    shift = (quarter - (2 * parity + p)) * tiles % LANES
+                    turned = pltpu.roll(dealt, shift, 1) if shift else dealt
+                    blocks.append(jnp.where(lanes // tiles == quarter, turned, 0.0))
+                high, rest = split(jnp.concatenate(blocks, axis=0))
+                rows = head * 2 * length
+                cols = slice(side * LANES, (side + 1) * LANES)
+                queries[source, c // per_group, rows : rows + 2 * length, cols] = high
+                queries[source, c // per_group, half_rows + rows : half_rows + rows + 2 * length, cols] = rest
+
+    def read(index):
+        source = order[index]
+        row = jnp.maximum(lax.div(table[source], 16) - 1, 0)
+        for g in range(groups):
+            product = jnp.dot(queries[source, g], matrices[row, g], preferred_element_type=F32)
+            product = product[:, :LANES] + product[:, LANES:]
+            product = product[:half_rows] + product[half_rows:]
+            for c in range(per_group):
+                tile = [
+                    product[(4 * c + part) * length : (4 * c + part + 1) * length] for part in range(4)
+                ]
+                even = tile[0] + pltpu.roll(tile[1], GROUP_WIDTH, 1)
+                odd = pltpu.roll(tile[2], GROUP_WIDTH, 1) + tile[3]
+                at = (g * per_group + c) * LANES
+                out[source, :, at : at + LANES] = jnp.where(low, even, odd)
+
+    loop(devices, lay_out)
+    loop(min(devices, matrices.shape[0]), read)
+
+
+def loop(trips, body):
+    pl.loop(0, trips, unroll=trips if trips <= 8 else 1)(body)
 
 
 def state_write_kernel(table, recv, after, store, out, keys, values, decays):
@@ -239,6 +317,10 @@
     return pltpu.with_memory_space_constraint(x, pltpu.VMEM)
 
 
+def in_hbm(x):
+    return pltpu.with_memory_space_constraint(x, pltpu.HBM)
+
+
 def in_smem(x):
     return pltpu.with_memory_space_constraint(x, pltpu.SMEM)
 
@@ -250,17 +332,27 @@
     tokens, channels = r.shape
     length = tokens // sessions
     width = 4 * channels + META
+    anywhere = pl.BlockSpec(memory_space=pltpu.HBM)
     send, route = pl.pallas_call(
         functools.partial(pack_kernel, store_rows),
         out_shape=(
             jax.ShapeDtypeStruct((devices, length, width), BF16),
             pltpu.SMEM((2 * sessions,), jnp.int32),
         ),
-        in_specs=[SMEM()] * 3 + [VMEM()] * 4,
-        out_specs=(VMEM(), SMEM()),
+        in_specs=[anywhere] * 7,
+        out_specs=(anywhere, SMEM()),
+        scratch_shapes=[
+            pltpu.SMEM(hold.shape, jnp.int32),
+            pltpu.SMEM(label.shape, jnp.int32),
+            pltpu.SMEM(count.shape, jnp.int32),
+            pltpu.VMEM((devices, length, META), BF16),
+            pltpu.VMEM((4, tokens, channels), BF16),
+            pltpu.SemaphoreType.DMA((7,)),
+            pltpu.SemaphoreType.DMA((4 * sessions + 1,)),
+        ],
         compiler_params=PARAMS,
         name="pack",
-    )(hold, label, count, r, k, v, w)
+    )(*(in_hbm(x) for x in (hold, label, count, r, k, v, w)))
     recv = in_vmem(lax.all_to_all(send, "cache", split_axis=0, concat_axis=0, tiled=True))
     part = pl.pallas_call(
         local_kernel,
@@ -272,18 +364,32 @@
         name="local",
     )(r, k, v, w, bonus.reshape(1, channels), send)
     resident = in_vmem(store)
+    groups, depth = heads // 8, 8 * state // LANES
+    matrices = pl.pallas_call(
+        retile_kernel,
+        out_shape=pltpu.VMEM((store_rows, groups, depth, 2 * LANES), BF16),
+        in_specs=[VMEM()] * 2,
+        out_specs=VMEM(),
+        scratch_shapes=[pltpu.VMEM((groups, depth, LANES), F32)],
+        cost_estimate=cost(8_000_000, 2_000_000),
+        compiler_params=PARAMS,
+        name="retile",
+    )(resident, in_vmem(part))
     back, table = pl.pallas_call(
         state_read_kernel,
         out_shape=(
             jax.ShapeDtypeStruct((devices, length, channels), F32),
             pltpu.SMEM((devices,), jnp.int32),
         ),
-        in_specs=[VMEM()] * 3,
+        in_specs=[VMEM()] * 2,
         out_specs=(VMEM(), SMEM()),
-        scratch_shapes=[pltpu.VMEM((heads * length, LANES), F32)] * 2,
+        scratch_shapes=[
+            pltpu.SMEM((devices,), jnp.int32),
+            pltpu.VMEM((devices, groups, 4 * 8 * length, depth), BF16),
+        ],
         compiler_params=PARAMS,
         name="state_read",
-    )(recv, resident, in_vmem(part))
+    )(recv, in_vmem(matrices))
     returned = in_vmem(lax.all_to_all(back, "cache", split_axis=0, concat_axis=0, tiled=True))
     updated = pl.pallas_call(
         state_write_kernel,

time: 50.6 us -> 40.6 us (0.80)
  local copies, waits for them, and re-layouts: 8.8 us -> 0.04 us
  Pallas kernels: 19.6 us -> 11.6 us
  waiting for transfers between devices: 10.5 us -> 16.9 us
    unnamed x32 -> x18, local copies, waits for them, and re-layouts: 8.8 us -> 0.04 us
    pallas_call x1, Pallas kernels: 7.87 us -> 1.83 us  [shards(): pl.pallas_call(state_read_kernel, out_shape=(jax.ShapeDtypeStruct((device...]
    all_to_all x1, waiting for transfers between devices: 0.01 us -> 3.47 us  [shards(): lax.all_to_all(back, 'cache', split_axis=0, concat_axis=0, tiled=True)]
    all_to_all x1, waiting for transfers between devices: 10.5 us -> 13.5 us  [shards(): lax.all_to_all(send, 'cache', split_axis=0, concat_axis=0, tiled=True)]
    pallas_call x1, Pallas kernels: 8.48 us -> 5.6 us  [shards(): pl.pallas_call(state_write_kernel, out_shape=jax.ShapeDtypeStruct(store.s...]
    pallas_call x1, Pallas kernels: 1.38 us -> 1.95 us  [shards(): pl.pallas_call(functools.partial(pack_kernel, store_rows), out_shape=(jax...]
  transfers between devices with their start and end apart: 2 -> 2, of which waited for: 1 -> 2; matrix products, arithmetic and copies ran while one was open for 0% -> 0% of each run, Pallas kernels for 19% -> 17%
where the time goes in v3:
time: 40.6 us; the launch traced here: 40.3 us
  waiting for transfers between devices  16.9 us (42%)
  Pallas kernels  11.6 us (29%)
  starting transfers between devices  11 us (27%)
  between operations  0.77 us (2%)
    all_to_all x1, waiting for transfers between devices, shards(): lax.all_to_all(send, 'cache', split_axis=0, concat_axis=0, tiled=True)  13.5 us
    all_to_all x1, starting transfers between devices, shards(): lax.all_to_all(send, 'cache', split_axis=0, concat_axis=0, tiled=True)  7.32 us
    pallas_call x1, Pallas kernels, shards(): pl.pallas_call(state_write_kernel, out_shape=jax.ShapeDtypeStruct(store.s...  5.6 us
    all_to_all x1, starting transfers between devices, shards(): lax.all_to_all(back, 'cache', split_axis=0, concat_axis=0, tiled=True)  3.64 us
    all_to_all x1, waiting for transfers between devices, shards(): lax.all_to_all(back, 'cache', split_axis=0, concat_axis=0, tiled=True)  3.47 us
    pallas_call x1, Pallas kernels, shards(): pl.pallas_call(functools.partial(pack_kernel, store_rows), out_shape=(jax...  1.95 us
    pallas_call x1, Pallas kernels, shards(): pl.pallas_call(state_read_kernel, out_shape=(jax.ShapeDtypeStruct((device...  1.83 us
    pallas_call x1, Pallas kernels, shards(): pl.pallas_call(local_kernel, out_shape=pltpu.VMEM((tokens, channels), F32...  0.96 us
  transfers between devices with their start and end apart: 2, of which 2 were waited for; matrix products, arithmetic and copies ran while one was open for 0% of the time, Pallas kernels for 17%

profile of v3, /device:TPU:0, one launch (start us, length us, event | category | flops | bytes accessed | tf_op | source)
XLA Modules:
  0.0 40.3 jit_solution(15564578054962895772)
XLA Ops:
  0.6 0.0 copy-start.4
  0.6 0.0 copy-start.3
  0.7 0.0 copy-start.2
  0.7 0.0 copy-start.1
  0.7 0.0 copy-start.6
  0.7 0.0 copy-start
  0.7 1.9 %pack.1 = (bf16[8,8,4224]{2,1,0:T(8,128)(2,1)}, s32[8]{0:T(128)S(4)}) custom-call(s32[40]{0:T(128)} %refs_0_.1, s32[4]{0:T(128)} %refs_1_.1, s32[4]{0:T(128)} %refs_2_.1, bf16[32,1024]{1,0:T(8,128)(2,1)} %r.1, bf16[32,1024]{1,0:T(8,128)(2,1)} %k.1, bf16[32,1024]{1,0:T(8,128)(2,1)} %v.1, bf16[32,1024]{1,0:T(8,128)(2,1)} %w.1), custom_call_target="tpu_custom_call" | custom-call | tf_op jit(solution)/shard_map/pack/pallas_call | solution.py:336
  2.7 7.3 %all-to-all-start = ((bf16[8,8,4224]{2,1,0:T(8,128)(2,1)}), bf16[8,8,4224]{2,1,0:T(8,128)(2,1)S(1)}, u32[]{:S(2)}, u32[]{:S(2)}) async-start(bf16[8,8,4224]{2,1,0:T(8,128)(2,1)} %get-tuple-element.7.after), calls=%async_computation | async-start | bytes 1081344 | tf_op jit(solution)/shard_map/all_to_all | solution.py:356
  10.0 0.0 copy-done.4
  10.0 0.0 copy-done.3
  10.0 0.0 copy-done.2
  10.0 0.0 copy-done.1
  10.0 0.0 copy-done.6
  10.0 1.0 %local.1.part = f32[32,1024]{1,0:T(8,128)S(1)} custom-call(bf16[32,1024]{1,0:T(8,128)(2,1)S(1)} %copy-done.1, bf16[32,1024]{1,0:T(8,128)(2,1)S(1)} %copy-done.2, bf16[32,1024]{1,0:T(8,128)(2,1)S(1)} %copy-done.3, bf16[32,1024]{1,0:T(8,128)(2,1)S(1)} %copy-done.4, f32[1,1024]{1,0:T(1,128)S(1)} %bitcast.3, bf16[8,8,4224]{2,1,0:T(8,128)(2,1)} %get-tuple-element.7.after), custom_call_target="tpu_custom_call" | custom-call | flops 8000000 | bytes 400000 | tf_op jit(solution)/shard_map/local/pallas_call | solution.py:357
  11.0 0.3 retile.1.matrices
  11.3 13.5 %all-to-all-done.recv = bf16[8,8,4224]{2,1,0:T(8,128)(2,1)S(1)} async-done(((bf16[8,8,4224]{2,1,0:T(8,128)(2,1)}), bf16[8,8,4224]{2,1,0:T(8,128)(2,1)S(1)}, u32[]{:S(2)}, u32[]{:S(2)}) %all-to-all-start) | async-done | bytes 540704 | tf_op jit(solution)/shard_map/all_to_all | solution.py:356
  24.8 1.8 %state_read.1 = (f32[8,8,1024]{2,1,0:T(8,128)}, s32[8]{0:T(128)S(4)}) custom-call(bf16[8,8,4224]{2,1,0:T(8,128)(2,1)S(1)} %all-to-all-done.recv, bf16[5,2,256,256]{3,2,1,0:T(8,128)(2,1)S(1)} %retile.1.matrices), custom_call_target="tpu_custom_call" | custom-call | tf_op jit(solution)/shard_map/state_read/pallas_call | solution.py:378
  26.6 3.6 %all-to-all-start.1 = ((f32[8,8,1024]{2,1,0:T(8,128)}), f32[8,8,1024]{2,1,0:T(8,128)S(1)}, u32[]{:S(2)}, u32[]{:S(2)}) async-start(f32[8,8,1024]{2,1,0:T(8,128)} %get-tuple-element.8.after), calls=%async_computation.1 | async-start | bytes 524288 | tf_op jit(solution)/shard_map/all_to_all | solution.py:393
  30.3 0.0 copy-start.7
  30.3 0.0 copy-start.8
  30.3 5.6 %state_write.1 = f32[5,16,4096]{2,1,0:T(8,128)} custom-call(s32[8]{0:T(128)S(4)} %get-tuple-element.9.table, bf16[8,8,4224]{2,1,0:T(8,128)(2,1)S(1)} %all-to-all-done.recv, f32[8,8,1024]{2,1,0:T(8,128)} %get-tuple-element.8.after, f32[5,16,4096]{2,1,0:T(8,128)S(1)} %copy-done), custom_call_target="tpu_custom_call" | custom-call | flops 8000000 | bytes 3000000 | tf_op jit(solution)/shard_map/state_write/pallas_call | solution.py:394
  35.9 3.5 %all-to-all-done.1.recv = f32[8,8,1024]{2,1,0:T(8,128)S(1)} async-done(((f32[8,8,1024]{2,1,0:T(8,128)}), f32[8,8,1024]{2,1,0:T(8,128)S(1)}, u32[]{:S(2)}, u32[]{:S(2)}) %all-to-all-start.1) | async-done | bytes 262176 | tf_op jit(solution)/shard_map/all_to_all | solution.py:393
  39.4 0.0 copy-done.7
  39.4 0.9 %finish.1 = bf16[32,1024]{1,0:T(8,128)(2,1)} custom-call(s32[8]{0:T(128)S(4)} %get-tuple-element.6.route, f32[8,8,1024]{2,1,0:T(8,128)S(1)} %all-to-all-done.1.recv, f32[32,1024]{1,0:T(8,128)S(1)} %local.1.part, bf16[32,1024]{1,0:T(8,128)(2,1)S(1)} %copy-done.5, f32[1,1024]{1,0:T(1,128)S(1)} %bitcast.4, f32[1,1024]{1,0:T(1,128)S(1)} %bitcast.5), custom_call_target="tpu_custom_call" | custom-call | tf_op jit(solution)/shard_map/finish/pallas_call | solution.py:404
  (4 shorter events, 0.0 us)
Async XLA Ops:
  0.6 9.3 %copy-start.4 = (bf16[32,1024]{1,0:T(8,128)(2,1)S(1)}, bf16[32,1024]{1,0:T(8,128)(2,1)}, u32[]{:S(2)}) copy-start(bf16[32,1024]{1,0:T(8,128)(2,1)} %w.1) | copy-start | bytes 196612
  0.6 9.3 %copy-start.3 = (bf16[32,1024]{1,0:T(8,128)(2,1)S(1)}, bf16[32,1024]{1,0:T(8,128)(2,1)}, u32[]{:S(2)}) copy-start(bf16[32,1024]{1,0:T(8,128)(2,1)} %v.1) | copy-start | bytes 196612
  0.7 9.3 %copy-start.2 = (bf16[32,1024]{1,0:T(8,128)(2,1)S(1)}, bf16[32,1024]{1,0:T(8,128)(2,1)}, u32[]{:S(2)}) copy-start(bf16[32,1024]{1,0:T(8,128)(2,1)} %k.1) | copy-start | bytes 196612
  0.7 9.3 %copy-start.1 = (bf16[32,1024]{1,0:T(8,128)(2,1)S(1)}, bf16[32,1024]{1,0:T(8,128)(2,1)}, u32[]{:S(2)}) copy-start(bf16[32,1024]{1,0:T(8,128)(2,1)} %r.1) | copy-start | bytes 196612
  0.7 9.3 %copy-start.6 = (f32[1024]{0:T(1024)S(1)}, f32[1024]{0:T(1024)}, u32[]{:S(2)}) copy-start(f32[1024]{0:T(1024)} %param.17) | copy-start | bytes 12292
  0.7 10.3 %copy-start = (f32[5,16,4096]{2,1,0:T(8,128)S(1)}, f32[5,16,4096]{2,1,0:T(8,128)}, u32[]{:S(2)}) copy-start(f32[5,16,4096]{2,1,0:T(8,128)} %store.3) | copy-start | bytes 3932164
  2.7 22.2 %all-to-all-start = ((bf16[8,8,4224]{2,1,0:T(8,128)(2,1)}), bf16[8,8,4224]{2,1,0:T(8,128)(2,1)S(1)}, u32[]{:S(2)}, u32[]{:S(2)}) async-start(bf16[8,8,4224]{2,1,0:T(8,128)(2,1)} %get-tuple-element.7.after), calls=%async_computation | async-start | bytes 1081344 | tf_op jit(solution)/shard_map/all_to_all | solution.py:356
  26.6 12.7 %all-to-all-start.1 = ((f32[8,8,1024]{2,1,0:T(8,128)}), f32[8,8,1024]{2,1,0:T(8,128)S(1)}, u32[]{:S(2)}, u32[]{:S(2)}) async-start(f32[8,8,1024]{2,1,0:T(8,128)} %get-tuple-element.8.after), calls=%async_computation.1 | async-start | bytes 524288 | tf_op jit(solution)/shard_map/all_to_all | solution.py:393
  30.3 9.1 %copy-start.5 = (bf16[32,1024]{1,0:T(8,128)(2,1)S(1)}, bf16[32,1024]{1,0:T(8,128)(2,1)}, u32[]{:S(2)}) copy-start(bf16[32,1024]{1,0:T(8,128)(2,1)} %gate.1) | copy-start | bytes 196612
  30.3 9.1 %copy-start.7 = (f32[1024]{0:T(1024)S(1)}, f32[1024]{0:T(1024)}, u32[]{:S(2)}) copy-start(f32[1024]{0:T(1024)} %param.18) | copy-start | bytes 12292
  30.3 9.1 %copy-start.8 = (f32[1024]{0:T(1024)S(1)}, f32[1024]{0:T(1024)}, u32[]{:S(2)}) copy-start(f32[1024]{0:T(1024)} %param.19) | copy-start | bytes 12292

commit v4 on v3

v4 whole, which is shorter than its diff:
```python
import functools

import jax
import jax.numpy as jnp
from jax import lax
from jax.experimental import pallas as pl
from jax.experimental.pallas import tpu as pltpu
from jax.sharding import PartitionSpec as P

GROUP_WIDTH = 64
EPS = 0.00064
LANES = 128
META = 128
F32 = jnp.float32
BF16 = jnp.bfloat16

SMEM = functools.partial(pl.BlockSpec, memory_space=pltpu.SMEM)
VMEM = functools.partial(pl.BlockSpec, memory_space=pltpu.VMEM)


def lane_ids(rows):
    return lax.broadcasted_iota(jnp.int32, (rows, LANES), 1)


def row_ids(rows):
    return lax.broadcasted_iota(jnp.int32, (rows, LANES), 0)


def place_of(hold, label, j, store_rows):
    location = hold[label[j]]
    owner = lax.div(location, jnp.int32(store_rows))
    return owner, location - owner * store_rows


def running_decay(w_tile):
    step = -jnp.exp(w_tile.astype(F32))
    rows = row_ids(step.shape[0])
    total = step
    shift = 1
    while shift < step.shape[0]:
        total = total + jnp.where(rows >= shift, pltpu.roll(total, shift, 0), 0.0)
        shift *= 2
    return step, total


def half_sums(x, low):
    first = jnp.sum(jnp.where(low, x, 0.0), axis=1, keepdims=True)
    second = jnp.sum(jnp.where(low, 0.0, x), axis=1, keepdims=True)
    return jnp.where(low, first, second)


def pack_kernel(store_rows, *refs):
    me, hold, label, count, *tensors = refs[:8]
    out, late, route, hold_in, label_in, count_in, meta, loaded, sems, sent = refs[8:]
    devices, length, _ = out.shape
    channels = tensors[0].shape[1]
    small = ((hold, hold_in), (label, label_in), (count, count_in))
    large = tuple((ref, loaded.at[index]) for index, ref in enumerate(tensors))
    loads = [
        pltpu.make_async_copy(source, target, sems.at[index])
        for index, (source, target) in enumerate(small + large)
    ]
    for load in loads:
        load.start()
    meta[...] = jnp.zeros(meta.shape, BF16)
    for load in loads[: len(small)]:
        load.wait()
    lanes = lane_ids(length)
    owners = []
    for j in range(label_in.shape[0]):
        owner, local = place_of(hold_in, label_in, j, store_rows)
        owners.append(owner)
        route[2 * j] = owner
        route[2 * j + 1] = count_in[j]
        tile = jnp.where(lanes == 0, local + 1, jnp.where(lanes == 1, count_in[j], 0))
        meta[owner] = tile.astype(F32).astype(BF16)
    sends = []

    def ship(source, target):
        sends.append(pltpu.make_async_copy(source, target, sent.at[len(sends)]))
        sends[-1].start()

    for index in range(4):
        loads[len(small) + index].wait()
        for j, owner in enumerate(owners):
            block = loaded.at[index, j * length : (j + 1) * length]
            at = slice(index % 2 * channels, (index % 2 + 1) * channels)
            if index < 2:
                ship(block, out.at[owner, :, at])
            else:
                slot = jnp.bitwise_xor(owner, me[0])
                slot = lax.rem(slot, devices // 2) * 2 + lax.div(slot, devices // 2)
                ship(block, late.at[slot, :, at])
    ship(meta, out.at[:, :, 2 * channels :])
    for send in sends:
        send.wait()


def collect_kernel(after, slots, *refs):
    del after
    near, out, sems = refs[:-2], refs[-2], refs[-1]
    copies = [
        pltpu.make_async_copy(source.at[1], out.at[index], sems.at[index])
        for index, source in enumerate((slots, *near))
    ]
    for copy in copies:
        copy.start()
    for copy in copies:
        copy.wait()


def read_meta(recv, base, table):
    for source in range(recv.shape[0]):
        tile = recv[source, :, base:].astype(F32)
        lanes = lane_ids(tile.shape[0])
        tile = jnp.where(lanes == 0, 16.0 * tile, jnp.where(lanes == 1, tile, 0.0))
        first = jnp.sum(jnp.where(row_ids(tile.shape[0]) == 0, tile, 0.0))
        table[source] = first.astype(jnp.int32)


def spread(scratch, column, tile, low, both):
    length = tile.shape[0]
    turned = pltpu.roll(tile, GROUP_WIDTH, 1)
    even = jnp.where(low, tile, turned) if both else tile
    odd = jnp.where(low, turned, tile) if both else turned
    scratch[pl.ds(2 * column * length, length), :] = even
    scratch[pl.ds((2 * column + 1) * length, length), :] = odd


def token_rows(length, group, t):
    return pl.ds(group * 8 * length + t, 8, stride=length)


def take(x, index):
    return jnp.take_along_axis(x, index, axis=1, mode="promise_in_bounds")


def split(x):
    high = x.astype(BF16)
    return high, (x - high.astype(F32)).astype(BF16)


def retile_kernel(store, part, out, resident, scratch):
    del part
    tiles = store.shape[2] // LANES

    @pl.loop(0, store.shape[0])
    def _(row):
        for g in range(store.shape[1] // 8):
            for tile in range(tiles):
                at = slice(tile * LANES, (tile + 1) * LANES)
                block = store[row, g * 8 : g * 8 + 8, at]
                scratch[g, tile * 8 : tile * 8 + 8, :] = block
                resident[row, g * 8 : g * 8 + 8, at] = block
            for head in range(8):
                for tile in range(0, tiles, 16):
                    halves = [
                        scratch[g, pl.ds(head + 8 * (tile + more), 8, stride=8), :] for more in (0, 8)
                    ]
                    high, low = split(jnp.concatenate(halves, axis=0))
                    at = slice(head * tiles + tile, head * tiles + tile + 16)
                    out[row, g, at, :LANES] = high
                    out[row, g, at, LANES:] = low


def deal_lanes(lanes, tiles):
    return (
        (lanes // GROUP_WIDTH) * GROUP_WIDTH + 2 * (lanes % tiles) + (lanes % GROUP_WIDTH) // tiles
    )


def block_diagonal(tile, column, target, deal, lanes, tiles):
    length = tile.shape[0]
    half_rows = 8 * 2 * length
    dealt = take(tile, deal)
    for parity in range(2):
        head = 2 * column + parity
        quarter, side = head % 4, head // 4
        blocks = []
        for p in range(2):
            shift = (quarter - (2 * parity + p)) * tiles % LANES
            turned = pltpu.roll(dealt, shift, 1) if shift else dealt
            blocks.append(jnp.where(lanes // tiles == quarter, turned, 0.0))
        high, rest = split(jnp.concatenate(blocks, axis=0))
        rows = head * 2 * length
        cols = slice(side * LANES, (side + 1) * LANES)
        target[rows : rows + 2 * length, cols] = high
        target[half_rows + rows : half_rows + rows + 2 * length, cols] = rest


def loop(trips, body):
    pl.loop(0, trips, unroll=trips if trips <= 8 else 1)(body)


def state_read_kernel(recv, matrices, out, table, order, places, queries, ready, taken, sems):
    devices, length, channels = out.shape
    columns = channels // LANES
    store_rows, groups, depth, _ = matrices.shape
    tiles = depth // 8
    per_group = columns // groups
    half_rows = 8 * 2 * length
    lanes = lane_ids(length)
    low = lanes < GROUP_WIDTH
    deal = deal_lanes(lanes, tiles)
    queries[...] = jnp.zeros(queries.shape, BF16)
    read_meta(recv, 2 * channels, table)

    served = jnp.int32(0)
    for row in range(store_rows):
        taken[row] = 0
    for source in range(devices):
        served = served + jnp.where(table[source] > 0, 1, 0)
    first, other = jnp.int32(0), served
    for source in range(devices):
        here = table[source] > 0
        order[jnp.where(here, first, other)] = jnp.int32(source)
        row = jnp.maximum(lax.div(table[source], 16) - 1, 0)
        places[jnp.where(here, first, store_rows)] = row
        taken[row] = jnp.where(here, 1, taken[row])
        first = first + jnp.where(here, 1, 0)
        other = other + jnp.where(here, 0, 1)
    for row in range(store_rows):
        free = taken[row] == 0
        places[jnp.where(free, first, store_rows)] = jnp.int32(row)
        first = first + jnp.where(free, 1, 0)
    places[store_rows] = served

    def lay_out(source):
        for c in range(columns):
            at = c * LANES
            step, total = running_decay(recv[source, :, channels + at : channels + at + LANES])
            decayed = recv[source, :, at : at + LANES].astype(F32) * jnp.exp(total - step)
            target = queries.at[source, c // per_group]
            block_diagonal(decayed, c % per_group, target, deal, lanes, tiles)

    def read(index):
        source = order[index]
        row = jnp.maximum(lax.div(table[source], 16) - 1, 0)
        for g in range(groups):
            product = jnp.dot(queries[source, g], matrices[row, g], preferred_element_type=F32)
            product = product[:, :LANES] + product[:, LANES:]
            product = product[:half_rows] + product[half_rows:]
            for c in range(per_group):
                tile = [
                    product[(4 * c + part) * length : (4 * c + part + 1) * length] for part in range(4)
                ]
                even = tile[0] + pltpu.roll(tile[1], GROUP_WIDTH, 1)
                odd = pltpu.roll(tile[2], GROUP_WIDTH, 1) + tile[3]
                at = (g * per_group + c) * LANES
                ready[index, :, at : at + LANES] = jnp.where(low, even, odd)
        block(index).start()

    def block(index):
        return pltpu.make_async_copy(ready.at[index], out.at[order[index]], sems.at[index])

    loop(devices, lay_out)
    loop(ready.shape[0], read)
    loop(ready.shape[0], lambda index: block(index).wait())


def scale_kernel(table, order, places, recv, store, after, out, gaps, decays):
    del after
    _, length, width = recv.shape
    channels = (width - META) // 2
    columns = channels // LANES
    store_rows, heads, _ = store.shape
    groups = heads // 8
    tiles = store.shape[2] // LANES
    low = lane_ids(length) < GROUP_WIDTH
    rows = row_ids(length)
    half = jnp.where(lane_ids(8) < GROUP_WIDTH, 0, 1)

    def scale(index):
        row = places[index]

        @pl.when(index < places[store_rows])
        def _():
            source = order[index]
            count = lax.rem(table[source], 16)
            for c in range(columns):
                at = c * LANES
                _, total = running_decay(recv[source, :, channels + at : channels + at + LANES])
                last = jnp.sum(jnp.where(rows == count - 1, total, 0.0), axis=0, keepdims=True)
                gap = jnp.exp(jnp.minimum(last - total, 0.0))
                gaps[source, :, at : at + LANES] = jnp.where(rows < count, gap, 0.0)
                spread(decays, c, jnp.broadcast_to(jnp.exp(last), (length, LANES)), low, False)
            for g in range(groups):
                decay = decays[token_rows(length, g, 0), :]
                for tile in range(tiles):
                    at = slice(tile * LANES, (tile + 1) * LANES)
                    out[row, g * 8 : g * 8 + 8, at] = (
                        take(decay, half + 2 * tile) * store[row, g * 8 : g * 8 + 8, at]
                    )

        @pl.when(index >= places[store_rows])
        def _():
            out[row] = store[row]

    pl.loop(0, store_rows)(scale)


def state_write_kernel(where, order, places, me, gaps, scaled, *refs):
    late, (out, keys, values, turned, result, sems) = refs[:-6], refs[-6:]
    devices, length, channels = gaps.shape
    columns = channels // LANES
    store_rows, heads, _ = scaled.shape
    groups = heads // 8
    tiles = scaled.shape[2] // LANES
    per_group = columns // groups
    half_rows = 8 * 2 * length
    lanes = lane_ids(length)
    low = lanes < GROUP_WIDTH
    deal = deal_lanes(lanes, tiles)
    keys[...] = jnp.zeros(keys.shape, BF16)

    for slot, (array, block) in enumerate(where):
        source = jnp.bitwise_xor(jnp.int32(slot), me[0])
        for c in range(columns):
            at = c * LANES
            column = c % per_group
            key = late[array][block, :, at : at + LANES].astype(F32) * gaps[source, :, at : at + LANES]
            block_diagonal(key, column, keys.at[slot, c // per_group], deal, lanes, tiles)
            value = late[array][block, :, channels + at : channels + at + LANES].astype(F32)
            other = pltpu.roll(value, GROUP_WIDTH, 1)
            for parity, (near, far) in enumerate(((value, other), (other, value))):
                pair = jnp.concatenate((jnp.where(low, near, 0.0), jnp.where(low, 0.0, far)), axis=0)
                for start in (0, half_rows):
                    at_row = start + (2 * column + parity) * 2 * length
                    values[slot, c // per_group, at_row : at_row + 2 * length, :] = pair.astype(BF16)

    def write(index):
        row = places[index]
        served = index < places[store_rows]
        slot = jnp.bitwise_xor(order[jnp.minimum(index, devices - 1)], me[0])
        for g in range(groups):
            product = lax.dot_general(
                keys[slot, g], values[slot, g], (((0,), (0,)), ((), ())), preferred_element_type=F32
            )
            for head in range(8):
                for tile in range(0, tiles, 8):
                    at = head * tiles + tile
                    turned[index % 2, g, pl.ds(head + 8 * tile, 8, stride=8), :] = product[at : at + 8]
            for tile in range(tiles):
                at = slice(tile * LANES, (tile + 1) * LANES)
                added = jnp.where(served, turned[index % 2, g, tile * 8 : tile * 8 + 8, :], 0.0)
                result[row, g * 8 : g * 8 + 8, at] = scaled[row, g * 8 : g * 8 + 8, at] + added
        flush(row).start()

    def flush(row):
        return pltpu.make_async_copy(result.at[row], out.at[row], sems.at[row])

    loop(store_rows, write)
    loop(store_rows, lambda row: flush(row).wait())


def local_kernel(r, k, v, w, bonus, after, out):
    del after
    length = 8
    sessions = r.shape[0] // length
    columns = r.shape[1] // LANES
    low = lane_ids(length) < GROUP_WIDTH
    rows = row_ids(length)

    @pl.loop(0, sessions)
    def _(j):
        at = pl.ds(pl.multiple_of(j * length, length), length)
        for c in range(columns):
            cols = slice(c * LANES, (c + 1) * LANES)
            step, total = running_decay(w[at, cols])
            query = r[at, cols].astype(F32)
            key = k[at, cols].astype(F32)
            value = v[at, cols].astype(F32)
            wkv = half_sums(query * bonus[:, cols] * key, low) * value
            decayed = query * jnp.exp(total - step)
            grown = key * jnp.exp(-total)
            for back in range(1, length):
                score = half_sums(decayed * pltpu.roll(grown, back, 0), low)
                wkv = wkv + jnp.where(rows >= back, score * pltpu.roll(value, back, 0), 0.0)
            out[at, cols] = wkv


def finish_kernel(route, recv, part, gate, gain, shift, out):
    _, length, channels = recv.shape
    low = lane_ids(length) < GROUP_WIDTH
    rows = row_ids(length)
    for j in range(out.shape[0] // length):
        owner, count = route[2 * j], route[2 * j + 1]
        at = slice(j * length, (j + 1) * length)
        for c in range(channels // LANES):
            cols = slice(c * LANES, (c + 1) * LANES)
            wkv = recv[owner, :, cols] + part[at, cols]
            centred = wkv - half_sums(wkv, low) * (1.0 / GROUP_WIDTH)
            variance = half_sums(centred * centred, low) * (1.0 / GROUP_WIDTH)
            normed = centred * lax.rsqrt(variance + EPS) * gain[:, cols] + shift[:, cols]
            g = gate[at, cols].astype(F32)
            gated = normed * (g / (1.0 + jnp.exp(-g)))
            out[at, cols] = jnp.where(rows < count, gated, 0.0).astype(BF16)


def cost(flops, nbytes):
    return pl.CostEstimate(flops=flops, bytes_accessed=nbytes, transcendentals=0)


PARAMS = pltpu.CompilerParams(vmem_limit_bytes=24 * 2**20)


def in_vmem(x):
    return pltpu.with_memory_space_constraint(x, pltpu.VMEM)


def in_hbm(x):
    return pltpu.with_memory_space_constraint(x, pltpu.HBM)


def in_smem(x):
    return pltpu.with_memory_space_constraint(x, pltpu.SMEM)


def step(r, k, v, w, gate, bonus, gain, shift, store, hold, label, count):
    devices = lax.axis_size("cache")
    sessions = label.shape[0]
    store_rows, heads, state = store.shape
    tokens, channels = r.shape
    length = tokens // sessions
    me = lax.axis_index("cache").astype(jnp.int32).reshape(1)
    hbm = pl.BlockSpec(memory_space=pltpu.HBM)
    anywhere = pl.BlockSpec(memory_space=pl.ANY)
    send, slots, route = pl.pallas_call(
        functools.partial(pack_kernel, store_rows),
        out_shape=(
            jax.ShapeDtypeStruct((devices, length, 2 * channels + META), BF16),
            jax.ShapeDtypeStruct((devices, length, 2 * channels), BF16),
            pltpu.SMEM((2 * sessions,), jnp.int32),
        ),
        in_specs=[SMEM()] + [hbm] * 7,
        out_specs=(hbm, anywhere, SMEM()),
        scratch_shapes=[
            pltpu.SMEM(hold.shape, jnp.int32),
            pltpu.SMEM(label.shape, jnp.int32),
            pltpu.SMEM(count.shape, jnp.int32),
            pltpu.VMEM((devices, length, META), BF16),
            pltpu.VMEM((4, tokens, channels), BF16),
            pltpu.SemaphoreType.DMA((7,)),
            pltpu.SemaphoreType.DMA((4 * sessions + 1,)),
        ],
        compiler_params=PARAMS,
        name="pack",
    )(me, *(in_hbm(x) for x in (hold, label, count, r, w, k, v)))
    recv = in_vmem(lax.all_to_all(send, "cache", split_axis=0, concat_axis=0, tiled=True))

    half = devices // 2
    arrays = [slots]
    where = {0: (0, 0)}
    for step in range(1, half):
        pair = slots[2 * step : 2 * step + 2]
        arrays.append(lax.ppermute(pair, "cache", [(i, i ^ step) for i in range(devices)]))
        where[step] = (step, 0)
    groups, depth = heads // 8, 8 * state // LANES
    matrices, resident = pl.pallas_call(
        retile_kernel,
        out_shape=(
            pltpu.VMEM((store_rows, groups, depth, 2 * LANES), BF16),
            pltpu.VMEM(store.shape, F32),
        ),
        in_specs=[VMEM(), hbm],
        out_specs=(VMEM(), VMEM()),
        scratch_shapes=[pltpu.VMEM((groups, depth, LANES), F32)],
        cost_estimate=cost(8_000_000, 2_000_000),
        compiler_params=PARAMS,
        name="retile",
    )(in_hbm(store), send)
    back, table, order, places = pl.pallas_call(
        state_read_kernel,
        out_shape=(
            jax.ShapeDtypeStruct((devices, length, channels), F32),
            pltpu.SMEM((devices,), jnp.int32),
            pltpu.SMEM((devices,), jnp.int32),
            pltpu.SMEM((store_rows + 1,), jnp.int32),
        ),
        in_specs=[VMEM()] * 2,
        out_specs=(hbm, SMEM(), SMEM(), SMEM()),
        scratch_shapes=[
            pltpu.VMEM((devices, groups, 4 * 8 * length, depth), BF16),
            pltpu.VMEM((min(devices, store_rows), length, channels), F32),
            pltpu.SMEM((store_rows,), jnp.int32),
            pltpu.SemaphoreType.DMA((min(devices, store_rows),)),
        ],
        compiler_params=PARAMS,
        name="state_read",
    )(recv, in_vmem(matrices))
    relay = pl.pallas_call(
        collect_kernel,
        out_shape=pltpu.VMEM((half, length, 2 * channels), BF16),
        in_specs=[anywhere] * (half + 1),
        out_specs=VMEM(),
        scratch_shapes=[pltpu.SemaphoreType.DMA((half,))],
        compiler_params=PARAMS,
        name="collect",
    )(back, *arrays)
    arrays.append(lax.ppermute(relay, "cache", [(i, i ^ half) for i in range(devices)]))
    for step in range(half):
        where[half + step] = (half, step)

    table, order, places = in_smem(table), in_smem(order), in_smem(places)
    returned = in_vmem(lax.all_to_all(back, "cache", split_axis=0, concat_axis=0, tiled=True))
    part = pl.pallas_call(
        local_kernel,
        out_shape=pltpu.VMEM((tokens, channels), F32),
        in_specs=[VMEM()] * 5 + [hbm],
        out_specs=VMEM(),
        cost_estimate=cost(8_000_000, 400_000),
        compiler_params=PARAMS,
        name="local",
    )(*(in_hbm(x) for x in (r, k, v, w, bonus.reshape(1, channels))), send)
    scaled, gaps = pl.pallas_call(
        scale_kernel,
        out_shape=(
            pltpu.VMEM(store.shape, F32),
            pltpu.VMEM((devices, length, channels), F32),
        ),
        in_specs=[SMEM()] * 3 + [VMEM()] * 2 + [hbm],
        out_specs=(VMEM(), VMEM()),
        scratch_shapes=[pltpu.VMEM((heads * length, LANES), F32)],
        cost_estimate=cost(8_000_000, 400_000),
        compiler_params=PARAMS,
        name="scale",
    )(table, order, places, recv, in_vmem(resident), back)
    updated = pl.pallas_call(
        functools.partial(state_write_kernel, [where[slot] for slot in range(devices)]),
        out_shape=jax.ShapeDtypeStruct(store.shape, F32),
        in_specs=[SMEM()] * 3 + [VMEM()] * (2 + len(arrays)),
        out_specs=hbm,
        scratch_shapes=[
            pltpu.VMEM((devices, groups, 4 * 8 * length, depth), BF16),
            pltpu.VMEM((devices, groups, 4 * 8 * length, LANES), BF16),
            pltpu.VMEM((2, groups, depth, LANES), F32),
            pltpu.VMEM(store.shape, F32),
            pltpu.SemaphoreType.DMA((store_rows,)),
        ],
        cost_estimate=cost(8_000_000, 3_000_000),
        compiler_params=PARAMS,
        name="state_write",
    )(order, places, me, in_vmem(gaps), in_vmem(scaled), *(in_vmem(x) for x in arrays))
    mixed = pl.pallas_call(
        finish_kernel,
        out_shape=jax.ShapeDtypeStruct((tokens, channels), BF16),
        in_specs=[SMEM()] + [VMEM()] * 5,
        out_specs=VMEM(),
        compiler_params=PARAMS,
        name="finish",
    )(
        in_smem(route),
        returned,
        in_vmem(part),
        in_vmem(gate),
        gain.reshape(1, channels),
        shift.reshape(1, channels),
    )
    return mixed, updated


def solution(mesh):
    rows = P(("groups", "cache"), "mp")
    states = P(("groups", "cache"), "mp", None)
    owned = P(("groups", "cache"))
    in_specs = (rows,) * 5 + (P("mp"),) * 3 + (states, P("groups"), owned, owned)
    return jax.shard_map(
        step, mesh=mesh, in_specs=in_specs, out_specs=(rows, states), check_vma=False
    )
```

time: 40.6 us -> 45.9 us (1.13)
  starting transfers between devices: 11 us -> 17 us
  waiting for transfers between devices: 16.9 us -> 15.5 us
  Pallas kernels: 11.6 us -> 12.2 us
    all_to_all x2, waiting for transfers between devices: 16.9 us -> 7.51 us  [the longest x1 7.51 us: step(): lax.all_to_all(send, 'cache', split_axis=0, concat_axis=0, tiled=True)]
    ppermute x0 -> x4, waiting for transfers between devices: none -> 8 us  [the longest x3 6.24 us: step(): lax.ppermute(pair, 'cache', [(i, i ^ step) for i in range(devices)])]
    ppermute x0 -> x4, starting transfers between devices: none -> 6.07 us  [the longest x3 3.63 us: step(): lax.ppermute(pair, 'cache', [(i, i ^ step) for i in range(devices)])]
    pallas_call x6 -> x8, Pallas kernels: 11.6 us -> 12.2 us  [the longest x1 2.04 us: step(): pl.pallas_call(functools.partial(state_write_kernel, [where[slot] for slo...]
  transfers between devices with their start and end apart: 2 -> 6, of which waited for: 2 -> 5; matrix products, arithmetic and copies ran while one was open for 0% -> 0% of each run, Pallas kernels for 17% -> 17%
where the time goes in v4:
time: 45.9 us; the launch traced here: 45.5 us
  starting transfers between devices  17 us (37%)
  waiting for transfers between devices  15.5 us (34%)
  Pallas kernels  12.2 us (27%)
  between operations  0.73 us (2%)
    all_to_all x1, waiting for transfers between devices, step(): lax.all_to_all(send, 'cache', split_axis=0, concat_axis=0, tiled=True)  7.51 us
    all_to_all x1, starting transfers between devices, step(): lax.all_to_all(send, 'cache', split_axis=0, concat_axis=0, tiled=True)  7.32 us
    ppermute x3, waiting for transfers between devices, step(): lax.ppermute(pair, 'cache', [(i, i ^ step) for i in range(devices)])  6.24 us
    ppermute x3, starting transfers between devices, step(): lax.ppermute(pair, 'cache', [(i, i ^ step) for i in range(devices)])  3.63 us
    all_to_all x1, starting transfers between devices, step(): lax.all_to_all(back, 'cache', split_axis=0, concat_axis=0, tiled=True)  3.62 us
    ppermute x1, starting transfers between devices, step(): lax.ppermute(relay, 'cache', [(i, i ^ half) for i in range(devices)])  2.44 us
    pallas_call x1, Pallas kernels, step(): pl.pallas_call(functools.partial(state_write_kernel, [where[slot] for slo...  2.04 us
    pallas_call x1, Pallas kernels, step(): pl.pallas_call(functools.partial(pack_kernel, store_rows), out_shape=(jax...  1.91 us
  transfers between devices with their start and end apart: 6, of which 5 were waited for; matrix products, arithmetic and copies ran while one was open for 0% of the time, Pallas kernels for 17%

profile of v4, /device:TPU:0, one launch (start us, length us, event | category | flops | bytes accessed | tf_op | source)
XLA Modules:
  0.0 45.5 jit_solution(14532209354701067793)
XLA Ops:
  0.6 1.9 %pack.1 = (bf16[8,8,2176]{2,1,0:T(8,128)(2,1)}, bf16[8,8,2048]{2,1,0:T(8,128)(2,1)S(1)}, s32[8]{0:T(128)S(4)}) custom-call(s32[1]{0:T(128)} %bitcast.refs_0_.me, s32[40]{0:T(128)} %refs_1_.1, s32[4]{0:T(128)} %refs_2_.1, s32[4]{0:T(128)} %refs_3_.1, bf16[32,1024]{1,0:T(8,128)(2,1)} %r.1, bf16[32,1024]{1,0:T(8,128)(2,1)} %w.1, bf16[32,1024]{1,0:T(8,128)(2,1)} %k.1, ...), custom_call_target="tpu_custom_call" | custom-call | tf_op jit(solution)/shard_map/pack/pallas_call | solution.py:428
  2.6 7.3 %all-to-all-start = ((bf16[8,8,2176]{2,1,0:T(8,128)(2,1)}), bf16[8,8,2176]{2,1,0:T(8,128)(2,1)S(1)}, u32[]{:S(2)}, u32[]{:S(2)}) async-start(bf16[8,8,2176]{2,1,0:T(8,128)(2,1)} %get-tuple-element.14.part.after), calls=%async_computation | async-start | bytes 557056 | tf_op jit(solution)/shard_map/all_to_all | solution.py:449
  9.9 1.7 %retile.1 = (bf16[5,2,256,256]{3,2,1,0:T(8,128)(2,1)S(1)}, f32[5,16,4096]{2,1,0:T(8,128)S(1)}) custom-call(f32[5,16,4096]{2,1,0:T(8,128)} %store.1, bf16[8,8,2176]{2,1,0:T(8,128)(2,1)} %get-tuple-element.14.part.after), custom_call_target="tpu_custom_call" | custom-call | flops 8000000 | bytes 2000000 | tf_op jit(solution)/shard_map/retile/pallas_call | solution.py:459
  11.6 7.5 %all-to-all-done.recv = bf16[8,8,2176]{2,1,0:T(8,128)(2,1)S(1)} async-done(((bf16[8,8,2176]{2,1,0:T(8,128)(2,1)}), bf16[8,8,2176]{2,1,0:T(8,128)(2,1)S(1)}, u32[]{:S(2)}, u32[]{:S(2)}) %all-to-all-start) | async-done | bytes 278560 | tf_op jit(solution)/shard_map/all_to_all | solution.py:449
  19.1 1.8 %state_read.1 = (f32[8,8,1024]{2,1,0:T(8,128)}, s32[8]{0:T(128)S(4)}, s32[8]{0:T(128)S(4)}, s32[6]{0:T(128)S(4)}) custom-call(bf16[8,8,2176]{2,1,0:T(8,128)(2,1)S(1)} %all-to-all-done.recv, bf16[5,2,256,256]{3,2,1,0:T(8,128)(2,1)S(1)} %get-tuple-element.15.matrices), custom_call_target="tpu_custom_call" | custom-call | tf_op jit(solution)/shard_map/state_read/pallas_call | solution.py:472
  20.9 3.6 %all-to-all-start.1 = ((f32[8,8,1024]{2,1,0:T(8,128)}), f32[8,8,1024]{2,1,0:T(8,128)S(1)}, u32[]{:S(2)}, u32[]{:S(2)}) async-start(f32[8,8,1024]{2,1,0:T(8,128)} %get-tuple-element.16.after), calls=%async_computation.1 | async-start | bytes 524288 | tf_op jit(solution)/shard_map/all_to_all | solution.py:505
  24.5 2.1 %collective-permute-start = (bf16[2,8,2048]{2,1,0:T(8,128)(2,1)S(1)}, bf16[2,8,2048]{2,1,0:T(8,128)(2,1)S(1)}, u32[]{:S(2)}, u32[]{:S(2)}) collective-permute-start(bf16[2,8,2048]{2,1,0:T(8,128)(2,1)S(1)} %get-tuple-element.26), channel_id=1, source_target_pairs={{0,2},{2,0},{4,6},{6,4},{8,10},{10,8},{12,14},{14,12},{1,3},{3,1},... | collective-permute-start | bytes 196616 | tf_op jit(solution)/shard_map/ppermute | solution.py:456
  26.6 1.5 %collective-permute-start.1 = (bf16[2,8,2048]{2,1,0:T(8,128)(2,1)S(1)}, bf16[2,8,2048]{2,1,0:T(8,128)(2,1)S(1)}, u32[]{:S(2)}, u32[]{:S(2)}) collective-permute-start(bf16[2,8,2048]{2,1,0:T(8,128)(2,1)S(1)} %get-tuple-element.25), channel_id=1, source_target_pairs={{0,4},{2,6},{4,0},{6,2},{8,12},{10,14},{12,8},{14,10},{1,5},{3,7},... | collective-permute-start | bytes 196616 | tf_op jit(solution)/shard_map/ppermute | solution.py:456
  28.1 0.1 collective-permute-start.2
  28.2 1.8 %collective-permute-done.refs_0_.refs_1_ = bf16[2,8,2048]{2,1,0:T(8,128)(2,1)S(1)} collective-permute-done((bf16[2,8,2048]{2,1,0:T(8,128)(2,1)S(1)}, bf16[2,8,2048]{2,1,0:T(8,128)(2,1)S(1)}, u32[]{:S(2)}, u32[]{:S(2)}) %collective-permute-start) | collective-permute-done | bytes 65568 | tf_op jit(solution)/shard_map/ppermute | solution.py:456
  30.0 3.5 %collective-permute-done.1.refs_1_.refs_2_ = bf16[2,8,2048]{2,1,0:T(8,128)(2,1)S(1)} collective-permute-done((bf16[2,8,2048]{2,1,0:T(8,128)(2,1)S(1)}, bf16[2,8,2048]{2,1,0:T(8,128)(2,1)S(1)}, u32[]{:S(2)}, u32[]{:S(2)}) %collective-permute-start.1) | collective-permute-done | bytes 65568 | tf_op jit(solution)/shard_map/ppermute | solution.py:456
  33.5 0.9 %collective-permute-done.2.refs_2_.refs_3_ = bf16[2,8,2048]{2,1,0:T(8,128)(2,1)S(1)} collective-permute-done((bf16[2,8,2048]{2,1,0:T(8,128)(2,1)S(1)}, bf16[2,8,2048]{2,1,0:T(8,128)(2,1)S(1)}, u32[]{:S(2)}, u32[]{:S(2)}) %collective-permute-start.2) | collective-permute-done | bytes 65568 | tf_op jit(solution)/shard_map/ppermute | solution.py:456
  34.4 0.2 collect.1
  34.6 2.4 %collective-permute-start.3 = (bf16[4,8,2048]{2,1,0:T(8,128)(2,1)S(1)}, bf16[4,8,2048]{2,1,0:T(8,128)(2,1)S(1)}, u32[]{:S(2)}, u32[]{:S(2)}) collective-permute-start(bf16[4,8,2048]{2,1,0:T(8,128)(2,1)S(1)} %collect.1), channel_id=1, source_target_pairs={{0,8},{2,10},{4,12},{6,14},{8,0},{10,2},{12,4},{14,6},{1,9},{3,11}... | collective-permute-start | bytes 393224 | tf_op jit(solution)/shard_map/ppermute | solution.py:500
  37.0 1.9 %local.1.part = f32[32,1024]{1,0:T(8,128)S(1)} custom-call(bf16[32,1024]{1,0:T(8,128)(2,1)} %r.1, bf16[32,1024]{1,0:T(8,128)(2,1)} %k.1, bf16[32,1024]{1,0:T(8,128)(2,1)} %v.1, bf16[32,1024]{1,0:T(8,128)(2,1)} %w.1, f32[1,1024]{1,0:T(1,128)} %bitcast.6, bf16[8,8,2176]{2,1,0:T(8,128)(2,1)} %get-tuple-element.14.part.after), custom_call_target="tpu_custom_call" | custom-call | flops 8000000 | bytes 400000 | tf_op jit(solution)/shard_map/local/pallas_call | solution.py:506
  39.0 1.8 %scale.1 = (f32[5,16,4096]{2,1,0:T(8,128)S(1)}, f32[8,8,1024]{2,1,0:T(8,128)S(1)}) custom-call(s32[8]{0:T(128)S(4)} %get-tuple-element.19.table, s32[8]{0:T(128)S(4)} %get-tuple-element.17.order, s32[6]{0:T(128)S(4)} %get-tuple-element.18.places, bf16[8,8,2176]{2,1,0:T(8,128)(2,1)S(1)} %all-to-all-done.recv, f32[5,16,4096]{2,1,0:T(8,128)S(1)} %get-tuple-element.20.store, ...), custom_call_target="tpu_custom_call" | custom-call | flops 8000000 | bytes 400000 | tf_op jit(solution)/shard_map/scale/pallas_call | solution.py:515
  40.7 1.8 %collective-permute-done.3.refs_4_ = bf16[4,8,2048]{2,1,0:T(8,128)(2,1)S(1)} collective-permute-done((bf16[4,8,2048]{2,1,0:T(8,128)(2,1)S(1)}, bf16[4,8,2048]{2,1,0:T(8,128)(2,1)S(1)}, u32[]{:S(2)}, u32[]{:S(2)}) %collective-permute-start.3) | collective-permute-done | bytes 131104 | tf_op jit(solution)/shard_map/ppermute | solution.py:500
  42.5 0.0 copy-start
  42.5 2.0 %state_write.1 = f32[5,16,4096]{2,1,0:T(8,128)} custom-call(s32[8]{0:T(128)S(4)} %get-tuple-element.17.order, s32[6]{0:T(128)S(4)} %get-tuple-element.18.places, s32[1]{0:T(128)} %bitcast.refs_0_.me, f32[8,8,1024]{2,1,0:T(8,128)S(1)} %get-tuple-element.21.gaps, f32[5,16,4096]{2,1,0:T(8,128)S(1)} %get-tuple-element.22.scaled, ...), custom_call_target="tpu_custom_call" | custom-call | flops 8000000 | bytes 3000000 | tf_op jit(solution)/shard_map/state_write/pallas_call | solution.py:528
  44.6 0.0 all-to-all-done.1.recv
  44.6 0.0 copy-done
  44.6 0.0 copy-done.1
  44.6 0.0 copy-done.2
  44.6 0.9 %finish.1 = bf16[32,1024]{1,0:T(8,128)(2,1)} custom-call(s32[8]{0:T(128)S(4)} %get-tuple-element.13.route, f32[8,8,1024]{2,1,0:T(8,128)S(1)} %all-to-all-done.1.recv, f32[32,1024]{1,0:T(8,128)S(1)} %local.1.part, bf16[32,1024]{1,0:T(8,128)(2,1)S(1)} %copy-done, f32[1,1024]{1,0:T(1,128)S(1)} %bitcast.4, f32[1,1024]{1,0:T(1,128)S(1)} %bitcast.5), custom_call_target="tpu_custom_call" | custom-call | tf_op jit(solution)/shard_map/finish/pallas_call | solution.py:544
  (3 shorter events, 0.0 us)
Async XLA Ops:
  2.6 16.6 %all-to-all-start = ((bf16[8,8,2176]{2,1,0:T(8,128)(2,1)}), bf16[8,8,2176]{2,1,0:T(8,128)(2,1)S(1)}, u32[]{:S(2)}, u32[]{:S(2)}) async-start(bf16[8,8,2176]{2,1,0:T(8,128)(2,1)} %get-tuple-element.14.part.after), calls=%async_computation | async-start | bytes 557056 | tf_op jit(solution)/shard_map/all_to_all | solution.py:449
  20.9 23.7 %all-to-all-start.1 = ((f32[8,8,1024]{2,1,0:T(8,128)}), f32[8,8,1024]{2,1,0:T(8,128)S(1)}, u32[]{:S(2)}, u32[]{:S(2)}) async-start(f32[8,8,1024]{2,1,0:T(8,128)} %get-tuple-element.16.after), calls=%async_computation.1 | async-start | bytes 524288 | tf_op jit(solution)/shard_map/all_to_all | solution.py:505
  24.5 5.4 %collective-permute-start = (bf16[2,8,2048]{2,1,0:T(8,128)(2,1)S(1)}, bf16[2,8,2048]{2,1,0:T(8,128)(2,1)S(1)}, u32[]{:S(2)}, u32[]{:S(2)}) collective-permute-start(bf16[2,8,2048]{2,1,0:T(8,128)(2,1)S(1)} %get-tuple-element.26), channel_id=1, source_target_pairs={{0,2},{2,0},{4,6},{6,4},{8,10},{10,8},{12,14},{14,12},{1,3},{3,1},... | collective-permute-start | bytes 196616 | tf_op jit(solution)/shard_map/ppermute | solution.py:456
  26.6 6.8 %collective-permute-start.1 = (bf16[2,8,2048]{2,1,0:T(8,128)(2,1)S(1)}, bf16[2,8,2048]{2,1,0:T(8,128)(2,1)S(1)}, u32[]{:S(2)}, u32[]{:S(2)}) collective-permute-start(bf16[2,8,2048]{2,1,0:T(8,128)(2,1)S(1)} %get-tuple-element.25), channel_id=1, source_target_pairs={{0,4},{2,6},{4,0},{6,2},{8,12},{10,14},{12,8},{14,10},{1,5},{3,7},... | collective-permute-start | bytes 196616 | tf_op jit(solution)/shard_map/ppermute | solution.py:456
  28.1 6.3 %collective-permute-start.2 = (bf16[2,8,2048]{2,1,0:T(8,128)(2,1)S(1)}, bf16[2,8,2048]{2,1,0:T(8,128)(2,1)S(1)}, u32[]{:S(2)}, u32[]{:S(2)}) collective-permute-start(bf16[2,8,2048]{2,1,0:T(8,128)(2,1)S(1)} %get-tuple-element.24), channel_id=1, source_target_pairs={{0,6},{2,4},{4,2},{6,0},{8,14},{10,12},{12,10},{14,8},{1,7},{3,5},... | collective-permute-start | bytes 196616 | tf_op jit(solution)/shard_map/ppermute | solution.py:456
  34.6 7.9 %collective-permute-start.3 = (bf16[4,8,2048]{2,1,0:T(8,128)(2,1)S(1)}, bf16[4,8,2048]{2,1,0:T(8,128)(2,1)S(1)}, u32[]{:S(2)}, u32[]{:S(2)}) collective-permute-start(bf16[4,8,2048]{2,1,0:T(8,128)(2,1)S(1)} %collect.1), channel_id=1, source_target_pairs={{0,8},{2,10},{4,12},{6,14},{8,0},{10,2},{12,4},{14,6},{1,9},{3,11}... | collective-permute-start | bytes 393224 | tf_op jit(solution)/shard_map/ppermute | solution.py:500
  42.5 2.1 %copy-start = (bf16[32,1024]{1,0:T(8,128)(2,1)S(1)}, bf16[32,1024]{1,0:T(8,128)(2,1)}, u32[]{:S(2)}) copy-start(bf16[32,1024]{1,0:T(8,128)(2,1)} %gate.1) | copy-start | bytes 196612
  42.5 2.1 %copy-start.1 = (f32[1024]{0:T(1024)S(1)}, f32[1024]{0:T(1024)}, u32[]{:S(2)}) copy-start(f32[1024]{0:T(1024)} %param.18) | copy-start | bytes 12292
  42.5 2.1 %copy-start.2 = (f32[1024]{0:T(1024)S(1)}, f32[1024]{0:T(1024)}, u32[]{:S(2)}) copy-start(f32[1024]{0:T(1024)} %param.19) | copy-start | bytes 12292
